TPU v7x, 512 devices: a whole 4x8x8 slice. The times are simulated.
512 devices in a mesh: ctx: 128 (over y, z, x_lo), fft: 4 (over x_hi, core).
Axes of the slice: x: 4 (x_hi: 2, x_lo: 2; x = x_hi * 2 + x_lo), y: 8, z: 8, core: 2. Of those that a mesh axis runs over, the one named last changes fastest.
Arguments:
- streams: bfloat16 [3, 16384, 2048], P(None, 'ctx', 'fft'), may hold values from -6 to 6
- taps: float32 [3, 7, 2048], P(None, None, 'fft'), may hold values from -2 to 2
- filters: bfloat16 [16384, 2048], P('ctx', 'fft')
- cotangent: bfloat16 [16384, 2048], P('ctx', 'fft')
Outputs:
- gated: bfloat16 [16384, 2048], P('ctx', 'fft')
- stream_grad: bfloat16 [3, 16384, 2048], P(None, 'ctx', 'fft')
- filter_grad: bfloat16 [16384, 2048], P('ctx', 'fft')
- tap_grad: float32 [3, 7, 2048], P(None, None, 'fft')
All inputs are finite; a program needn't handle non-finite values.
Results may differ from a plain program's by a relative error of at most 0.012.
Values may be sent and summed in bfloat16 or wider, within the bound.
A program may use at most 64 MiB of HBM per device.

v0:
```python
import math

import jax
import jax.numpy as jnp
from jax import lax
from jax.sharding import PartitionSpec as P

exact_mode = lax.Precision.HIGHEST


def shifted(value, axis, steps):
    count = lax.axis_size(axis)
    first, last = (max(0, -steps), min(count, count - steps))
    return lax.ppermute(value, axis, [(source, source + steps) for source in range(first, last)])


def angle_table(row_count, col_count, col_start, period):
    row_ids = lax.iota(jnp.int32, row_count)
    col_ids = col_start + lax.iota(jnp.int32, col_count)
    turns = row_ids[:, None] * col_ids[None, :] % period
    angles = turns.astype(jnp.float32) * (2.0 * math.pi / period)
    return (jnp.cos(angles), jnp.sin(angles))


def column_start(col_count):
    return lax.axis_index("fft") * col_count


def split_product(table, signal):
    high_part = table.astype(jnp.bfloat16)
    low_part = (table - high_part.astype(jnp.float32)).astype(jnp.bfloat16)
    first = jnp.einsum("kt,ctu->cku", high_part, signal, preferred_element_type=jnp.float32)
    second = jnp.einsum("kt,ctu->cku", low_part, signal, preferred_element_type=jnp.float32)
    return first + second


def forward_transform(signal):
    input_rows = signal.shape[1]
    row_count = 2 * input_rows
    col_count = signal.shape[2]
    full_width = col_count * lax.axis_size("fft")
    period = row_count * full_width
    cos_first, sin_first = angle_table(row_count, input_rows, 0, row_count)
    first_re = split_product(cos_first, signal)
    first_im = -split_product(sin_first, signal)
    cos_twist, sin_twist = angle_table(row_count, col_count, column_start(col_count), period)
    turned_re = first_re * cos_twist + first_im * sin_twist
    turned_im = first_im * cos_twist - first_re * sin_twist
    turned_re, turned_im = (
        lax.all_to_all(turned_re, "fft", split_axis=1, concat_axis=2, tiled=True),
        lax.all_to_all(turned_im, "fft", split_axis=1, concat_axis=2, tiled=True),
    )
    cos_second, sin_second = angle_table(full_width, full_width, 0, full_width)
    spec_re = jnp.einsum("cut,tk->cuk", turned_re, cos_second, precision=exact_mode) + jnp.einsum(
        "cut,tk->cuk", turned_im, sin_second, precision=exact_mode
    )
    spec_im = jnp.einsum("cut,tk->cuk", turned_im, cos_second, precision=exact_mode) - jnp.einsum(
        "cut,tk->cuk", turned_re, sin_second, precision=exact_mode
    )
    return (spec_re, spec_im)


def inverse_transform(spec_re, spec_im, keep_rows):
    full_width = spec_re.shape[2]
    cos_second, sin_second = angle_table(full_width, full_width, 0, full_width)
    back_re = jnp.einsum("cuk,kt->cut", spec_re, cos_second, precision=exact_mode) - jnp.einsum(
        "cuk,kt->cut", spec_im, sin_second, precision=exact_mode
    )
    back_im = jnp.einsum("cuk,kt->cut", spec_im, cos_second, precision=exact_mode) + jnp.einsum(
        "cuk,kt->cut", spec_re, sin_second, precision=exact_mode
    )
    back_re, back_im = (
        lax.all_to_all(
            back_re.astype(jnp.bfloat16), "fft", split_axis=2, concat_axis=1, tiled=True
        ).astype(back_re.dtype),
        lax.all_to_all(
            back_im.astype(jnp.bfloat16), "fft", split_axis=2, concat_axis=1, tiled=True
        ).astype(back_im.dtype),
    )
    row_count = back_re.shape[1]
    col_count = back_re.shape[2]
    period = row_count * full_width
    cos_twist, sin_twist = angle_table(row_count, col_count, column_start(col_count), period)
    turned_re = back_re * cos_twist - back_im * sin_twist
    turned_im = back_im * cos_twist + back_re * sin_twist
    cos_first, sin_first = angle_table(keep_rows, row_count, 0, row_count)
    result = jnp.einsum("tk,cku->ctu", cos_first, turned_re, precision=exact_mode) - jnp.einsum(
        "tk,cku->ctu", sin_first, turned_im, precision=exact_mode
    )
    return result * (1.0 / period)


def regroup_out(stacked):
    count_here = stacked.shape[0]
    channel_count = stacked.shape[1]
    block_rows = stacked.shape[2]
    shaped = stacked.reshape(count_here, 1, channel_count, 1, block_rows)
    arrived = lax.all_to_all(
        lax.all_to_all(shaped, "ctx", split_axis=2, concat_axis=3, tiled=True),
        "fft",
        split_axis=4,
        concat_axis=1,
        tiled=True,
    )
    return arrived.reshape(
        count_here, arrived.shape[1] * arrived.shape[2], arrived.shape[3], arrived.shape[4]
    )


def regroup_back(stacked):
    count_here = stacked.shape[0]
    groups = lax.axis_size("fft")
    shaped = stacked.reshape(
        count_here, groups, stacked.shape[1] // groups, stacked.shape[2], stacked.shape[3]
    )
    arrived = lax.all_to_all(
        lax.all_to_all(shaped, "ctx", split_axis=3, concat_axis=2, tiled=True),
        "fft",
        split_axis=1,
        concat_axis=4,
        tiled=True,
    )
    return arrived.reshape(count_here, arrived.shape[2], arrived.shape[4])


def merged(block):
    return block.reshape(block.shape[0] * block.shape[1], block.shape[2], block.shape[3])


def local(streams, taps, filters, cotangent):
    block_rows = streams.shape[1]
    tap_reach = taps.shape[1] - 1
    earlier = shifted(streams[:, block_rows - tap_reach :, :], "ctx", 1)
    extended = jnp.concatenate([earlier, streams], axis=1).astype(jnp.float32)
    convolved = jnp.zeros((3, block_rows, streams.shape[2]), jnp.float32)
    for offset in range(tap_reach + 1):
        convolved = (
            convolved
            + taps[:, offset, None, :]
            * extended[:, tap_reach - offset : tap_reach - offset + block_rows, :]
        )
    query_side = convolved[0]
    key_side = convolved[1]
    value_side = convolved[2]
    product = (key_side * value_side).astype(jnp.bfloat16)
    seq_total = block_rows * lax.axis_size("ctx")
    scale_factor = 1.0 / math.sqrt(seq_total)
    arrived = regroup_out(jnp.stack([product, filters]).swapaxes(1, 2))
    per_stream = arrived.shape[1]
    grid_rows = arrived.shape[2]
    first_re, first_im = forward_transform(merged(arrived))
    prod_re = first_re[:per_stream]
    prod_im = first_im[:per_stream]
    filt_re = first_re[per_stream:]
    filt_im = first_im[per_stream:]
    mixed_re = prod_re * filt_re - prod_im * filt_im
    mixed_im = prod_re * filt_im + prod_im * filt_re
    mixed_cols = inverse_transform(mixed_re, mixed_im, grid_rows).astype(jnp.bfloat16)
    mixed_back = regroup_back(mixed_cols.reshape(1, per_stream, grid_rows, mixed_cols.shape[2]))
    mixed = mixed_back[0].T.astype(jnp.float32)
    gated = (query_side * mixed).astype(jnp.bfloat16)
    upstream = cotangent.astype(jnp.float32)
    mixed_grad = (upstream * query_side).astype(jnp.bfloat16)
    query_grad = upstream * mixed
    grad_cols = regroup_out(mixed_grad.T[None])
    grad_re, grad_im = forward_transform(merged(grad_cols))
    through_re = filt_re * grad_re + filt_im * grad_im
    through_im = filt_re * grad_im - filt_im * grad_re
    lagged_re = prod_re * grad_re + prod_im * grad_im
    lagged_im = prod_re * grad_im - prod_im * grad_re
    both_times = inverse_transform(
        jnp.concatenate([through_re, lagged_re], axis=0),
        jnp.concatenate([through_im, lagged_im], axis=0),
        grid_rows,
    )
    product_grad_cols = both_times[:per_stream].astype(jnp.bfloat16)
    filter_grad_cols = (both_times[per_stream:] * scale_factor).astype(jnp.bfloat16)
    returned = regroup_back(jnp.stack([product_grad_cols, filter_grad_cols]))
    product_grad = returned[0].T.astype(jnp.float32)
    filter_grad = returned[1].T
    conv_grad = jnp.stack([query_grad, product_grad * value_side, product_grad * key_side])
    following = shifted(conv_grad[:, :tap_reach, :].astype(jnp.bfloat16), "ctx", -1).astype(
        jnp.float32
    )
    extended_grad = jnp.concatenate([conv_grad, following], axis=1)
    running = jnp.zeros((3, block_rows, streams.shape[2]), jnp.float32)
    for offset in range(tap_reach + 1):
        running = (
            running + taps[:, offset, None, :] * extended_grad[:, offset : offset + block_rows, :]
        )
    stream_grad = running.astype(jnp.bfloat16)
    tap_terms = jnp.stack(
        [
            jnp.sum(
                conv_grad * extended[:, tap_reach - offset : tap_reach - offset + block_rows, :],
                axis=1,
            )
            for offset in range(tap_reach + 1)
        ],
        axis=1,
    )
    tap_grad = lax.psum(tap_terms, "ctx") * scale_factor
    return (gated, stream_grad, filter_grad, tap_grad)


def solution(mesh):
    in_specs = (P(None, "ctx", "fft"), P(None, None, "fft"), P("ctx", "fft"), P("ctx", "fft"))
    out_specs = (P("ctx", "fft"), P(None, "ctx", "fft"), P("ctx", "fft"), P(None, None, "fft"))
    return jax.shard_map(local, mesh=mesh, in_specs=in_specs, out_specs=out_specs, check_vma=False)
```

profile of v0, /device:TPU:6, one launch (start us, length us, event | category | flops | bytes accessed | tf_op | source)
XLA Modules:
  0.0 968.6 jit_solution(4194647207119168019)
XLA Ops:
  12.4 19.5 %all-to-all-start.8 = ((bf16[128,2,256]{2,1,0:T(2,128)(2,1)}), bf16[128,2,256]{2,1,0:T(2,128)(2,1)S(1)}, u32[]{:S(2)}, u32[]{:S(2)}) async-start(bf16[128,2,256]{2,1,0:T(2,128)(2,1)} %reshape.134), calls=%async_computation.8 | async-start | bytes 262144 | tf_op jit(solution)/shard_map/all_to_all | solution.py:99
  32.1 11.6 %all-to-all-done.8 = bf16[128,2,256]{2,1,0:T(2,128)(2,1)S(1)} async-done(((bf16[128,2,256]{2,1,0:T(2,128)(2,1)}), bf16[128,2,256]{2,1,0:T(2,128)(2,1)S(1)}, u32[]{:S(2)}, u32[]{:S(2)}) %all-to-all-start.8) | async-done | bytes 131104 | tf_op jit(solution)/shard_map/all_to_all | solution.py:99
  44.6 4.8 all-to-all-start.9
  52.4 6.6 all-to-all-start
  61.1 12.9 %all-to-all-done = bf16[2,1,512,1,128]{4,0,3,1,2:T(2,128)(2,1)S(1)} async-done(((bf16[2,1,512,1,128]{4,0,3,1,2:T(2,128)(2,1)}), bf16[2,1,512,1,128]{4,0,3,1,2:T(2,128)(2,1)S(1)}, u32[]{:S(2)}, u32[]{:S(2)}) %all-to-all-start) | async-done | bytes 262176 | tf_op jit(solution)/shard_map/all_to_all | solution.py:99
  75.0 7.5 all-to-all-start.1
  91.0 4.8 all-to-all-start.10
  103.0 7.2 all-to-all-start.11
  117.5 4.9 reshape.126
  122.4 5.1 all-to-all-start.2
  131.9 4.9 reshape.124
  153.5 5.3 all-to-all-start.3
  180.4 5.6 reduce.3
  195.5 5.2 fusion.92
  218.6 4.8 all-to-all-start.4
  241.9 5.0 all-to-all-start.5
  251.2 6.6 all-to-all-start.12
  265.0 6.6 all-to-all-start.13
  283.5 7.0 all-to-all-start.6
  304.0 15.1 %all-to-all-start.14 = ((bf16[128,2,512]{2,1,0:T(2,128)(2,1)}), bf16[128,2,512]{2,1,0:T(2,128)(2,1)S(1)}, u32[]{:S(2)}, u32[]{:S(2)}) async-start(bf16[128,2,512]{2,1,0:T(2,128)(2,1)} %reshape.144), calls=%async_computation.14 | async-start | bytes 524288 | tf_op jit(solution)/shard_map/all_to_all | solution.py:117
  320.4 13.2 %all-to-all-done.14 = bf16[128,2,512]{2,1,0:T(2,128)(2,1)S(1)} async-done(((bf16[128,2,512]{2,1,0:T(2,128)(2,1)}), bf16[128,2,512]{2,1,0:T(2,128)(2,1)S(1)}, u32[]{:S(2)}, u32[]{:S(2)}) %all-to-all-start.14) | async-done | bytes 262176 | tf_op jit(solution)/shard_map/all_to_all | solution.py:117
  345.0 6.4 all-to-all-start.7
  356.2 601.0 %psum.7 = f32[3,7,512]{2,0,1:T(4,128)S(1)} all-reduce(f32[3,7,512]{2,0,1:T(4,128)S(1)} %constant_dynamic-update-slice_fusion), channel_id=1, replica_groups=mesh['ctx'=128,'fft'=4] {'ctx'}, use_global_device_ids=true, to_apply=%region_7.8 | all-reduce | flops 10752 | bytes 86016 | tf_op jit(solution)/shard_map/psum | solution.py:202
  957.2 7.9 collective-permute-start.1
  (190 shorter events, 187.2 us)
Async XLA Ops:
  1.4 6.0 collective-permute-start
  9.5 40.0 %copy-start.3 = (f32[3,128,512]{2,1,0:T(8,128)}, f32[3,128,512]{2,1,0:T(8,128)S(1)}, u32[]{:S(2)}) copy-start(f32[3,128,512]{2,1,0:T(8,128)S(1)} %multiply_add_fusion.1) | copy-start | bytes 2359300
  9.5 40.0 %copy-start.13 = (bf16[128,512]{1,0:T(8,128)(2,1)S(1)}, bf16[128,512]{1,0:T(8,128)(2,1)}, u32[]{:S(2)}) copy-start(bf16[128,512]{1,0:T(8,128)(2,1)} %param.6) | copy-start | bytes 393220
  12.4 31.3 %all-to-all-start.8 = ((bf16[128,2,256]{2,1,0:T(2,128)(2,1)}), bf16[128,2,256]{2,1,0:T(2,128)(2,1)S(1)}, u32[]{:S(2)}, u32[]{:S(2)}) async-start(bf16[128,2,256]{2,1,0:T(2,128)(2,1)} %reshape.134), calls=%async_computation.8 | async-start | bytes 262144 | tf_op jit(solution)/shard_map/all_to_all | solution.py:99
  44.6 7.8 all-to-all-start.9
  52.4 21.6 %all-to-all-start = ((bf16[2,1,512,1,128]{4,0,3,1,2:T(2,128)(2,1)}), bf16[2,1,512,1,128]{4,0,3,1,2:T(2,128)(2,1)S(1)}, u32[]{:S(2)}, u32[]{:S(2)}) async-start(bf16[2,1,512,1,128]{4,0,3,1,2:T(2,128)(2,1)} %copy.137), calls=%async_computation | async-start | bytes 524288 | tf_op jit(solution)/shard_map/all_to_all | solution.py:99
  75.0 16.0 %all-to-all-start.1 = ((bf16[2,1,4,128,128]{3,2,1,0,4:T(4,128)(2,1)}), bf16[2,1,4,128,128]{3,2,1,0,4:T(4,128)(2,1)}, u32[]{:S(2)}, u32[]{:S(2)}) async-start(bf16[2,1,4,128,128]{3,2,1,0,4:T(4,128)(2,1)} %copy.139), calls=%async_computation.1 | async-start | bytes 524288 | tf_op jit(solution)/shard_map/all_to_all | solution.py:98
  91.0 12.0 %all-to-all-start.10 = ((f32[4,1,32768]{2,1,0:T(1,128)}), f32[4,1,32768]{2,1,0:T(1,128)S(1)}, u32[]{:S(2)}, u32[]{:S(2)}) async-start(f32[4,1,32768]{2,1,0:T(1,128)} %reshape.136), calls=%async_computation.10 | async-start | bytes 1048576 | tf_op jit(solution)/shard_map/all_to_all | solution.py:50
  103.0 19.4 %all-to-all-start.11 = ((f32[4,1,32768]{2,1,0:T(1,128)}), f32[4,1,32768]{2,1,0:T(1,128)}, u32[]{:S(2)}, u32[]{:S(2)}) async-start(f32[4,1,32768]{2,1,0:T(1,128)} %reshape.138), calls=%async_computation.11 | async-start | bytes 1048576 | tf_op jit(solution)/shard_map/all_to_all | solution.py:51
  122.4 31.1 %all-to-all-start.2 = ((f32[4,1,65536]{2,1,0:T(1,128)}), f32[4,1,65536]{2,1,0:T(1,128)}, u32[]{:S(2)}, u32[]{:S(2)}) async-start(f32[4,1,65536]{2,1,0:T(1,128)} %reshape.126), calls=%async_computation.2 | async-start | bytes 2097152 | tf_op jit(solution)/shard_map/all_to_all | solution.py:50
  153.5 26.9 %all-to-all-start.3 = ((f32[4,1,65536]{2,1,0:T(1,128)}), f32[4,1,65536]{2,1,0:T(1,128)}, u32[]{:S(2)}, u32[]{:S(2)}) async-start(f32[4,1,65536]{2,1,0:T(1,128)} %reshape.124), calls=%async_computation.3 | async-start | bytes 2097152 | tf_op jit(solution)/shard_map/all_to_all | solution.py:51
  218.6 23.3 %all-to-all-start.4 = ((bf16[4,2,16384]{2,1,0:T(2,128)(2,1)}), bf16[4,2,16384]{2,1,0:T(2,128)(2,1)}, u32[]{:S(2)}, u32[]{:S(2)}) async-start(bf16[4,2,16384]{2,1,0:T(2,128)(2,1)} %reshape.130), calls=%async_computation.4 | async-start | bytes 524288 | tf_op jit(solution)/shard_map/all_to_all | solution.py:73
  241.9 9.3 all-to-all-start.5
  251.2 13.8 %all-to-all-start.12 = ((bf16[4,2,32768]{2,1,0:T(2,128)(2,1)}), bf16[4,2,32768]{2,1,0:T(2,128)(2,1)S(1)}, u32[]{:S(2)}, u32[]{:S(2)}) async-start(bf16[4,2,32768]{2,1,0:T(2,128)(2,1)} %reshape.142), calls=%async_computation.12 | async-start | bytes 1048576 | tf_op jit(solution)/shard_map/all_to_all | solution.py:73
  265.0 17.7 %all-to-all-start.13 = ((bf16[4,2,32768]{2,1,0:T(2,128)(2,1)}), bf16[4,2,32768]{2,1,0:T(2,128)(2,1)S(1)}, u32[]{:S(2)}, u32[]{:S(2)}) async-start(bf16[4,2,32768]{2,1,0:T(2,128)(2,1)} %reshape.140), calls=%async_computation.13 | async-start | bytes 1048576 | tf_op jit(solution)/shard_map/all_to_all | solution.py:76
  283.5 20.5 %all-to-all-start.6 = ((bf16[128,2,256]{2,1,0:T(2,128)(2,1)}), bf16[128,2,256]{2,1,0:T(2,128)(2,1)}, u32[]{:S(2)}, u32[]{:S(2)}) async-start(bf16[128,2,256]{2,1,0:T(2,128)(2,1)} %reshape.132), calls=%async_computation.6 | async-start | bytes 262144 | tf_op jit(solution)/shard_map/all_to_all | solution.py:117
  304.0 29.6 %all-to-all-start.14 = ((bf16[128,2,512]{2,1,0:T(2,128)(2,1)}), bf16[128,2,512]{2,1,0:T(2,128)(2,1)S(1)}, u32[]{:S(2)}, u32[]{:S(2)}) async-start(bf16[128,2,512]{2,1,0:T(2,128)(2,1)} %reshape.144), calls=%async_computation.14 | async-start | bytes 524288 | tf_op jit(solution)/shard_map/all_to_all | solution.py:117
  335.9 9.2 all-to-all-start.15
  340.7 13.8 %copy-start.12 = (bf16[128,512]{1,0:T(8,128)(2,1)S(1)}, bf16[128,512]{1,0:T(8,128)(2,1)}, u32[]{:S(2)}) copy-start(bf16[128,512]{1,0:T(8,128)(2,1)} %param.7) | copy-start | bytes 393220
  345.0 9.4 all-to-all-start.7
  356.0 610.7 %copy-start.15 = (f32[3,512]{1,0:T(4,128)S(1)}, f32[3,512]{1,0:T(4,128)}, u32[]{:S(2)}) copy-start(f32[3,512]{1,0:T(4,128)} %copy-done.14) | copy-start | bytes 18436
  356.0 610.7 %copy-start.17 = (f32[3,512]{1,0:T(4,128)S(1)}, f32[3,512]{1,0:T(4,128)}, u32[]{:S(2)}) copy-start(f32[3,512]{1,0:T(4,128)} %copy-done.16) | copy-start | bytes 18436
  356.0 610.7 %copy-start.19 = (f32[3,1,512]{2,0,1:T(4,128)S(1)}, f32[3,1,512]{2,0,1:T(4,128)}, u32[]{:S(2)}) copy-start(f32[3,1,512]{2,0,1:T(4,128)} %copy-done.18) | copy-start | bytes 18436
  957.2 9.4 collective-permute-start.1
  (14 other events, 63.0 us)
where the time goes:
time: 979 us; the launch traced here: 969 us
  blocking collectives  601 us (61%)
  starting transfers between devices  129 us (13%)
  local copies, waits for them, and re-layouts  103 us (11%)
  waiting for transfers between devices  55.3 us (6%)
  matrix products  55 us (6%)
  other arithmetic  22.8 us (2%)
    psum x1, blocking collectives, local(): tap_grad = lax.psum(tap_terms, 'ctx') * scale_factor  601 us
    unnamed x75, local copies, waits for them, and re-layouts  43.2 us
    all_to_all x2, starting transfers between devices, regroup_out(): lax.all_to_all(shaped, 'ctx', split_axis=2, concat_axis=3, tiled=True)  26.1 us
    all_to_all x2, waiting for transfers between devices, regroup_out(): lax.all_to_all(shaped, 'ctx', split_axis=2, concat_axis=3, tiled=True)  24.5 us
    all_to_all x2, starting transfers between devices, regroup_back(): lax.all_to_all(shaped, 'ctx', split_axis=3, concat_axis=2, tiled=True)  22.1 us
  transfers between devices with their start and end apart: 18, of which 11 were waited for; matrix products, arithmetic and copies ran while one was open for 13% of the time, Pallas kernels for 0%

commit v1 on v0

v1 whole, which is shorter than its diff:
```python
import functools
import math

import jax
import jax.numpy as jnp
import numpy as np
from jax import lax
from jax.experimental import pallas as pl
from jax.experimental.pallas import tpu as pltpu
from jax.sharding import PartitionSpec as P

MESH = pl.DeviceIdType.MESH
VMEM = pltpu.VMEM


def exchange_kernel(count, shared, *refs):
    number = len(shared)
    sources, targets, (send_sem, recv_sem, own_sem) = refs[:number], refs[number : 2 * number], refs[2 * number :]
    me = lax.axis_index("ctx")
    barrier = pltpu.get_barrier_semaphore()

    def greet(step, carry):
        peer = lax.rem(me + step, count)
        pl.semaphore_signal(barrier, inc=1, device_id={"ctx": peer}, device_id_type=MESH)
        return carry

    lax.fori_loop(1, count, greet, 0)
    own = [
        pltpu.make_async_copy(source if whole else source.at[me], target.at[me], own_sem.at[i])
        for i, (source, target, whole) in enumerate(zip(sources, targets, shared))
    ]
    for copy in own:
        copy.start()
    pl.semaphore_wait(barrier, count - 1)

    def send(step, carry):
        peer = lax.rem(me + step, count)
        for i, (source, target, whole) in enumerate(zip(sources, targets, shared)):
            pltpu.make_async_remote_copy(
                source if whole else source.at[peer],
                target.at[me],
                send_sem.at[i],
                recv_sem.at[i],
                device_id={"ctx": peer},
                device_id_type=MESH,
            ).start()
        return carry

    lax.fori_loop(1, count, send, 0)
    for copy in own:
        copy.wait()
    for i, target in enumerate(targets):
        others = target.at[pl.ds(0, count - 1)]
        whole = pltpu.make_async_remote_copy(
            others, others, send_sem.at[i], recv_sem.at[i], device_id={"ctx": me}, device_id_type=MESH
        )
        whole.wait_send()
        whole.wait_recv()


def exchange(arrays, shared, collective_id):
    count = lax.axis_size("ctx")
    outs = [
        jax.ShapeDtypeStruct((count,) + tuple(a.shape) if whole else a.shape, a.dtype)
        for a, whole in zip(arrays, shared)
    ]
    number = len(arrays)
    return pl.pallas_call(
        functools.partial(exchange_kernel, count, shared),
        out_shape=outs,
        in_specs=[pl.BlockSpec(memory_space=VMEM)] * number,
        out_specs=[pl.BlockSpec(memory_space=VMEM)] * number,
        scratch_shapes=[pltpu.SemaphoreType.DMA((number,))] * 3,
        compiler_params=pltpu.CompilerParams(collective_id=collective_id, has_side_effects=True),
    )(*arrays)


def tables(a_size, b_size):
    k1, a, b, k2 = (np.arange(n, dtype=np.int64) for n in (a_size, a_size, b_size, b_size))
    first = (4 * k1[:, None] + 1) * a[None, :] % (4 * a_size) / (4.0 * a_size)
    twist = (4 * k1[:, None] + 1) * b[None, :] % (4 * a_size * b_size) / (4.0 * a_size * b_size)
    second = b[:, None] * k2[None, :] % b_size / float(b_size)
    return [np.exp(-2j * np.pi * x).astype(np.complex64) for x in (first, twist, second)]


def owner_math(streams, filters, cotangent, taps):
    _, chans, a_size, b_size = streams.shape
    total = a_size * b_size
    reach = taps.shape[1] - 1
    first, twist, second = tables(a_size, b_size)
    dot = functools.partial(jnp.einsum, precision=lax.Precision.HIGHEST, preferred_element_type=jnp.float32)
    e1 = np.concatenate([first.real, first.imag], 0)
    e2 = np.block([[second.real, second.imag], [-second.imag, second.real]])
    back = np.concatenate([first.real.T, first.imag.T], 1) / total
    twr, twi = jnp.asarray(twist.real), jnp.asarray(twist.imag)

    def forward(x):
        y = dot("ka,cab->ckb", jnp.asarray(e1), x.astype(jnp.float32))
        re, im = y[:, :a_size], y[:, a_size:]
        turned = jnp.concatenate([re * twr - im * twi, re * twi + im * twr], -1)
        z = dot("ckb,bq->ckq", turned, jnp.asarray(e2))
        return z[..., :b_size], z[..., b_size:]

    def inverse(re, im):
        u = dot("ckq,bq->ckb", jnp.concatenate([re, im], -1), jnp.asarray(e2))
        ur, ui = u[..., :b_size], u[..., b_size:]
        turned = jnp.concatenate([ur * twr + ui * twi, ui * twr - ur * twi], 1)
        return dot("ak,ckb->cab", jnp.asarray(back), turned)

    flat = streams.astype(jnp.float32).reshape(3, chans, total)
    wide = jnp.pad(flat, ((0, 0), (0, 0), (reach, 0)))
    shifts = [wide[..., reach - j : reach - j + total] for j in range(reach + 1)]
    query, key, value = sum(taps[:, j, :, None] * shifts[j] for j in range(reach + 1))
    upstream = cotangent.astype(jnp.float32).reshape(chans, total)
    grid = (chans, a_size, b_size)
    pr, pi = forward((key * value).astype(jnp.bfloat16).reshape(grid))
    fr, fi = forward(filters)
    gr, gi = forward((upstream * query).astype(jnp.bfloat16).reshape(grid))
    mixed = inverse(pr * fr - pi * fi, pr * fi + pi * fr).astype(jnp.bfloat16).astype(jnp.float32).reshape(chans, total)
    pgrad = inverse(fr * gr + fi * gi, fr * gi - fi * gr).astype(jnp.bfloat16).astype(jnp.float32).reshape(chans, total)
    scale = 1.0 / math.sqrt(total)
    fgrad = (inverse(pr * gr + pi * gi, pr * gi - pi * gr) * scale).astype(jnp.bfloat16)
    gated = (query * mixed).astype(jnp.bfloat16).reshape(grid)
    cgrad = jnp.stack([upstream * mixed, pgrad * value, pgrad * key])
    after = jnp.pad(cgrad, ((0, 0), (0, 0), (0, reach)))
    sgrad = sum(taps[:, j, :, None] * after[..., j : j + total] for j in range(reach + 1)).astype(jnp.bfloat16)
    tgrad = jnp.stack([jnp.sum(cgrad * shifts[j], axis=-1) for j in range(reach + 1)], 1) * scale
    return gated, sgrad.reshape((3,) + grid), fgrad, tgrad


def local(streams, taps, filters, cotangent):
    rows, width = filters.shape
    owners = lax.axis_size("ctx")
    chans = width // owners
    everything = jnp.concatenate([streams, filters[None], cotangent[None]], 0)
    outgoing = everything.swapaxes(1, 2).reshape(5, owners, chans, rows).swapaxes(0, 1)
    (arrived,) = exchange([outgoing], (False,), 0)
    grid = arrived.transpose(1, 2, 0, 3)
    mine = lax.dynamic_slice_in_dim(taps, lax.axis_index("ctx") * chans, chans, 2)
    gated, sgrad, fgrad, tgrad = owner_math(grid[:3], grid[3], grid[4], mine)
    results = jnp.concatenate([gated[None], sgrad, fgrad[None]], 0).transpose(2, 0, 1, 3)
    small = jnp.pad(tgrad.reshape(1, -1), ((0, 0), (0, 128 - tgrad.size)))
    back, tall = exchange([results, small], (False, True), 1)
    back = back.swapaxes(0, 1).reshape(5, width, rows).swapaxes(1, 2)
    tap_grad = tall[:, 0, : tgrad.size].reshape((owners,) + tgrad.shape).transpose(1, 2, 0, 3).reshape(taps.shape)
    return back[0], back[1:4], back[4], tap_grad


def solution(mesh):
    in_specs = (P(None, "ctx", "fft"), P(None, None, "fft"), P("ctx", "fft"), P("ctx", "fft"))
    out_specs = (P("ctx", "fft"), P(None, "ctx", "fft"), P("ctx", "fft"), P(None, None, "fft"))
    return jax.shard_map(local, mesh=mesh, in_specs=in_specs, out_specs=out_specs, check_vma=False)
```

time: 979 us -> 111 us (0.11)
  blocking collectives: 601 us -> 0 us
  starting transfers between devices: 129 us -> 0 us
  local copies, waits for them, and re-layouts: 103 us -> 17.7 us
  Pallas kernels: 0 us -> 67.7 us
  waiting for transfers between devices: 55.3 us -> 0 us
  matrix products: 55 us -> 9.52 us
    psum x1 -> x0, blocking collectives: 601 us -> none  [local(): tap_grad = lax.psum(tap_terms, 'ctx') * scale_factor]
    all_to_all x16 -> x0, starting transfers between devices: 117 us -> none  [the longest x2 26.1 us: regroup_out(): lax.all_to_all(shaped, 'ctx', split_axis=2, concat_axis=3, tiled=True)]
    pallas_call x0 -> x2, Pallas kernels: none -> 67.7 us  [exchange(): pl.pallas_call(functools.partial(exchange_kernel, count, shared), out_sha...]
    all_to_all x16 -> x0, waiting for transfers between devices: 54.3 us -> none  [the longest x2 24.5 us: regroup_out(): lax.all_to_all(shaped, 'ctx', split_axis=2, concat_axis=3, tiled=True)]
    dot_general x28 -> x12, matrix products: 55 us -> 9.52 us  [the longest x3 2.99 us: forward(): z = dot('ckb,bq->ckq', turned, jnp.asarray(e2))]
    unnamed x75 -> x48, local copies, waits for them, and re-layouts: 43.2 us -> 8.36 us
    all_to_all x23 -> x0, local copies, waits for them, and re-layouts: 20.9 us -> none  [the longest x2 7.3 us: forward_transform(): lax.all_to_all(turned_im, 'fft', split_axis=1, concat_axis=2, tiled=True)]
    convert_element_type x12 -> x0, local copies, waits for them, and re-layouts: 20.6 us -> none  [the longest x8 13.8 us: inverse_transform(): back_re, back_im = (lax.all_to_all(back_re.astype(jnp.bfloat16), 'fft', s...]
  transfers between devices with their start and end apart: 18 -> 0, of which waited for: 11 -> 0; matrix products, arithmetic and copies ran while one was open for 13% -> 0% of each run, Pallas kernels for 0% -> 0%
where the time goes in v1:
time: 111 us; the launch traced here: 110 us
  Pallas kernels  67.7 us (61%)
  local copies, waits for them, and re-layouts  17.7 us (16%)
  other arithmetic  14.2 us (13%)
  matrix products  9.52 us (9%)
  between operations  1.19 us (1%)
    pallas_call x2, Pallas kernels, exchange(): pl.pallas_call(functools.partial(exchange_kernel, count, shared), out_sha...  67.7 us
    unnamed x48, local copies, waits for them, and re-layouts  8.36 us
    reduce_sum x2, other arithmetic, owner_math(): jnp.sum(cgrad * shifts[j], axis=-1)  3.36 us
    dot_general x3, matrix products, forward(): z = dot('ckb,bq->ckq', turned, jnp.asarray(e2))  2.99 us
    add x1, other arithmetic, owner_math(): sum((taps[:, j, :, None] * shifts[j] for j in range(reach + 1)))  2.52 us
    reshape x1, other arithmetic, owner_math(): return (gated, sgrad.reshape((3,) + grid), fgrad, tgrad)  2.52 us
    dot_general x3, matrix products, inverse(): return dot('ak,ckb->cab', jnp.asarray(back), turned)  2.45 us

profile of v1, /device:TPU:6, one launch (start us, length us, event | category | flops | bytes accessed | tf_op | source)
XLA Modules:
  0.0 110.3 jit_solution(11167284209149397202)
XLA Ops:
  0.6 1.1 constant_dynamic-slice_fusion.5
  1.8 1.2 %copy.94 = bf16[3,128,512]{1,2,0:T(8,128)(2,1)S(1)} copy(bf16[3,128,512]{2,1,0:T(8,128)(2,1)} %param.9) | data formatting | bytes 786432 | tf_op args[0]
  3.0 1.0 copy.92
  4.0 1.0 copy.93
  5.2 1.1 copy.165
  6.2 36.7 %shard_map.120 = bf16[128,5,4,128]{3,2,1,0:T(4,128)(2,1)} custom-call(bf16[128,5,4,128]{3,2,1,0:T(4,128)(2,1)} %bitcast.133), custom_call_target="tpu_custom_call" | custom-call | tf_op jit(solution)/shard_map/pallas_call | solution.py:68
  43.0 1.3 %copy.164 = bf16[128,5,4,128]{3,2,0,1:T(4,128)(2,1)S(1)} copy(bf16[128,5,4,128]{3,2,1,0:T(4,128)(2,1)} %shard_map.120) | data formatting | bytes 1310720 | tf_op jit(solution)/shard_map/pallas_call | solution.py:68
  44.4 2.5 %multiply_add_fusion = f32[3,4,16384]{2,1,0:T(4,128)S(1)} fusion(f32[3,4,16384]{2,1,0:T(4,128)S(1)} %convert_bitcast_fusion, f32[3,4]{1,0:T(4,128)S(1)} %get-tuple-element.66, f32[3,4]{1,0:T(4,128)S(1)} %get-tuple-element.67, f32[3,4]{1,0:T(4,128)S(1)} %get-tuple-element.68, f32[3,4]{1,0:T(4,128)S(1)} %get-tuple-element.69, ...), kind=kLoop, calls=%fused_computation.21 | loop fusion | flops 2555904 | bytes 1573200 | tf_op jit(solution)/shard_map/add | solution.py:113
  48.5 1.0 fusion.5
  49.5 1.0 fusion.9
  51.5 1.3 %fusion.3 = f32[4,128,128]{2,1,0:T(8,128)} fusion(f32[128,256,1]{1,0,2:T(8,128)S(1)} %copy-done.2, f32[4,128,128]{1,2,0:T(8,128)S(1)} %get-tuple-element.42, f32[4,128,128]{1,2,0:T(8,128)S(1)} %get-tuple-element.41), kind=kOutput, calls=%fused_computation.9 | convolution fusion | flops 201588736 | bytes 917504 | tf_op jit(solution)/shard_map/ak,ckb->cab/dot_general | solution.py:108
  52.7 1.8 %copy.144 = f32[4,128,128]{1,0,2:T(4,128)} copy(f32[4,128,128]{2,1,0:T(8,128)} %fusion.3) | data formatting | bytes 524288
  54.5 1.8 %fusion.44 = (bf16[1,4,128,128]{3,1,0,2:T(4,128)(2,1)}, bf16[4,128,128]{2,0,1:T(4,128)(2,1)S(1)}) fusion(f32[4,128,128]{1,0,2:T(4,128)} %copy.144, f32[3,4,16384]{2,1,0:T(4,128)S(1)} %multiply_add_fusion, bf16[5,4,128,128]{3,1,2,0:T(4,128)(2,1)S(1)} %bitcast.126), kind=kLoop, calls=%fused_computation.92 | loop fusion | flops 327680 | bytes 917504 | tf_op jit(solution)/shard_map/convert_element_type | solution.py:123
  56.3 1.3 %convolution_bitcast_fusion = f32[4,256,128]{1,2,0:T(8,128)S(1)} fusion(f32[256,128,1]{1,0,2:T(8,128)} %constant.39, bf16[4,128,128]{2,0,1:T(4,128)(2,1)S(1)} %get-tuple-element.38), kind=kOutput, calls=%fused_computation | convolution fusion | flops 201326592 | bytes 786432 | tf_op jit(solution)/shard_map/ka,cab->ckb/dot_general | solution.py:98
  57.7 1.0 fusion.20
  60.2 0.8 multiply_add_fusion.3
  62.6 1.1 slice_multiply_fusion
  64.4 3.0 %multiply_reduce_fusion = (f32[3,4]{1,0:T(4,128)S(1)}, f32[3,4]{1,0:T(4,128)S(1)}, f32[3,4]{1,0:T(4,128)S(1)}, f32[3,4]{1,0:T(4,128)S(1)}, f32[3,4]{1,0:T(4,128)...) fusion(f32[3,4,16384]{2,1,0:T(4,128)S(1)} %convert_bitcast_fusion, f32[1,4,16384]{2,1,0:T(4,128)S(1)} %get-tuple-element.31, ...), kind=kLoop, calls=%fused_computation.14 | loop fusion | flops 2752440 | bytes 2359584 | tf_op jit(solution)/shard_map/reduce_sum | solution.py:127
  68.9 2.5 %copy_bitcast_fusion.2 = bf16[3,4,128,128]{3,1,0,2:T(4,128)(2,1)S(1)} fusion(f32[3,4]{1,0:T(4,128)S(1)} %get-tuple-element.66, f32[3,4]{1,0:T(4,128)S(1)} %get-tuple-element.67, f32[3,4]{1,0:T(4,128)S(1)} %get-tuple-element.68, f32[3,4]{1,0:T(4,128)S(1)} %get-tuple-element.69, f32[3,4]{1,0:T(4,128)S(1)} %copy-done.13, ...), kind=kLoop, calls=%fused_computation.59 | loop fusion | flops 2752512 | bytes 1179984 | tf_op jit(solution)/shard_map/reshape | solution.py:128
  72.2 1.3 %maximum_bitcast_fusion.refs_0_ = bf16[128,5,4,128]{3,2,1,0:T(4,128)(2,1)} fusion(bf16[1,4,128,128]{3,1,0,2:T(4,128)(2,1)S(1)} %bitcast.137, bf16[3,4,128,128]{3,1,0,2:T(4,128)(2,1)S(1)} %copy_bitcast_fusion.2, bf16[1,4,128,128]{3,1,0,2:T(4,128)(2,1)S(1)} %copy-done.11), kind=kLoop, calls=%fused_computation.23 | loop fusion | flops 655360 | bytes 1310720 | tf_op jit(solution)/shard_map/transpose | solution.py:141
  73.6 31.0 %shard_map.121 = (bf16[128,5,4,128]{3,2,1,0:T(4,128)(2,1)}, f32[128,1,128]{2,1,0:T(1,128)}) custom-call(bf16[128,5,4,128]{3,2,1,0:T(4,128)(2,1)} %maximum_bitcast_fusion.refs_0_, f32[1,128]{1,0:T(1,128)} %pad.14.refs_1_), custom_call_target="tpu_custom_call" | custom-call | tf_op jit(solution)/shard_map/pallas_call | solution.py:68
  104.5 0.9 copy.123
  106.0 1.6 %reshape.109 = f32[3,7,512]{2,1,0:T(8,128)} reshape(f32[3,7,128,4]{3,2,1,0:T(8,128)S(1)} %copy.124) | data formatting | bytes 86016 | tf_op jit(solution)/shard_map/reshape | solution.py:145
  107.8 0.9 copy.126
  (81 shorter events, 10.9 us)
Async XLA Ops:
  1.7 42.6 %copy-start.12 = (f32[3,4]{1,0:T(4,128)}, f32[3,4]{1,0:T(4,128)S(1)}, u32[]{:S(2)}) copy-start(f32[3,4]{1,0:T(4,128)S(1)} %get-tuple-element.70) | copy-start | bytes 148
  1.7 42.6 %copy-start.14 = (f32[3,4]{1,0:T(4,128)}, f32[3,4]{1,0:T(4,128)S(1)}, u32[]{:S(2)}) copy-start(f32[3,4]{1,0:T(4,128)S(1)} %get-tuple-element.71) | copy-start | bytes 148
  1.8 42.6 %copy-start.16 = (f32[3,1,4]{2,0,1:T(4,128)}, f32[3,1,4]{2,0,1:T(4,128)S(1)}, u32[]{:S(2)}) copy-start(f32[3,1,4]{2,0,1:T(4,128)S(1)} %copy.166) | copy-start | bytes 148
  44.4 2.6 %copy-start.4 = (f32[256,128,1]{1,0,2:T(8,128)S(1)}, f32[256,128,1]{1,0,2:T(8,128)}, u32[]{:S(2)}) copy-start(f32[256,128,1]{1,0,2:T(8,128)} %constant.39) | copy-start | bytes 393220
  46.9 1.0 copy-start.6
  46.9 1.0 copy-start.8
  47.5 1.0 copy-start
  50.6 0.9 copy-start.2
  54.5 3.1 %copy-start.7 = (f32[128,128]{0,1:T(8,128)S(1)}, f32[128,128]{0,1:T(8,128)}, u32[]{:S(2)}) copy-start(f32[128,128]{0,1:T(8,128)} %constant.28.clone) | copy-start | bytes 196612
  54.5 3.1 %copy-start.9 = (f32[128,128]{0,1:T(8,128)S(1)}, f32[128,128]{0,1:T(8,128)}, u32[]{:S(2)}) copy-start(f32[128,128]{0,1:T(8,128)} %constant.29.clone) | copy-start | bytes 196612
  60.2 0.9 copy-start.3
  61.7 2.0 %copy-start.1 = (f32[4,128,128]{1,0,2:T(4,128)S(1)}, f32[4,128,128]{1,0,2:T(4,128)}, u32[]{:S(2)}) copy-start(f32[4,128,128]{1,0,2:T(4,128)} %copy.144) | copy-start | bytes 786436
  64.4 4.6 %copy-start.13 = (f32[3,4]{1,0:T(4,128)S(1)}, f32[3,4]{1,0:T(4,128)}, u32[]{:S(2)}) copy-start(f32[3,4]{1,0:T(4,128)} %copy-done.12) | copy-start | bytes 148
  64.4 4.6 %copy-start.15 = (f32[3,4]{1,0:T(4,128)S(1)}, f32[3,4]{1,0:T(4,128)}, u32[]{:S(2)}) copy-start(f32[3,4]{1,0:T(4,128)} %copy-done.14) | copy-start | bytes 148
  64.4 4.6 %copy-start.17 = (f32[3,1,4]{2,0,1:T(4,128)S(1)}, f32[3,1,4]{2,0,1:T(4,128)}, u32[]{:S(2)}) copy-start(f32[3,1,4]{2,0,1:T(4,128)} %copy-done.16) | copy-start | bytes 148
  64.4 7.1 %copy-start.5 = (f32[4,128,128]{1,2,0:T(8,128)S(1)}, f32[4,128,128]{1,2,0:T(8,128)}, u32[]{:S(2)}) copy-start(f32[4,128,128]{1,2,0:T(8,128)} %get-tuple-element.56) | copy-start | bytes 786436
  67.4 4.8 %copy-start.11 = (bf16[1,4,128,128]{3,1,0,2:T(4,128)(2,1)S(1)}, bf16[1,4,128,128]{3,1,0,2:T(4,128)(2,1)}, u32[]{:S(2)}) copy-start(bf16[1,4,128,128]{3,1,0,2:T(4,128)(2,1)} %get-tuple-element.37) | copy-start | bytes 393220
  105.5 2.1 %copy-start.10 = (bf16[128,5,4,128]{3,2,1,0:T(4,128)(2,1)S(1)}, bf16[128,5,4,128]{3,2,1,0:T(4,128)(2,1)}, u32[]{:S(2)}) copy-start(bf16[128,5,4,128]{3,2,1,0:T(4,128)(2,1)} %get-tuple-element.6) | copy-start | bytes 1966084

commit v2 on v1

v2 whole, which is shorter than its diff:
```python
import math

import jax
import jax.numpy as jnp
import numpy as np
from jax import lax
from jax.experimental import pallas as pl
from jax.experimental.pallas import tpu as pltpu
from jax.sharding import PartitionSpec as P

MESH = pl.DeviceIdType.MESH
VMEM = pltpu.VMEM
F32 = jnp.float32
BF16 = jnp.bfloat16
CHANS = 4
TILE = 128
ENTRIES = 24


def halves(table):
    high = table.astype(BF16)
    return high, (table - high.astype(np.float64)).astype(BF16)


def make_tables(a_size, b_size):
    k1, a, b, k2 = (np.arange(n, dtype=np.int64) for n in (a_size, a_size, b_size, b_size))
    first = (4 * k1[:, None] + 1) * a[None, :] % (4 * a_size) / (4.0 * a_size)
    twist = (4 * k1[:, None] + 1) * b[None, :] % (4 * a_size * b_size) / (4.0 * a_size * b_size)
    second = b[:, None] * k2[None, :] % b_size / float(b_size)
    first, twist, second = (np.exp(-2j * np.pi * x) for x in (first, twist, second))
    e1 = np.concatenate([first.real, first.imag], 0)
    e2 = np.block([[second.real, second.imag], [-second.imag, second.real]])
    back = np.concatenate([first.real.T, first.imag.T], 1) / (a_size * b_size)
    e1 = np.concatenate(halves(e1), 1)
    e2, e2t, back = (np.stack(halves(x)) for x in (e2, e2.T, back))
    twist = np.stack([np.tile(x, (1, 2)) for x in (twist.real, twist.imag)]).astype(np.float32)
    return e1, e2, e2t, back, twist


def dot(a, b):
    return jnp.dot(a, b, preferred_element_type=F32)


def split(x):
    high = x.astype(BF16)
    return high, (x - high.astype(F32)).astype(BF16)


def block_kernel(
    streams_hbm, filters_hbm, cot_hbm, taps_hbm, e1_hbm, e2_hbm, e2t_hbm, back_hbm, tw_hbm, taps_s,
    gated_ref, sgrad_ref, fgrad_ref, tgrad_ref,
    st, fl, ct, taps, e1, e2, e2t, back, tw,
    snd1, snd2, rcv1, rcv2, grid, shifts, qkv, spec, rows, ret_snd, ret_rcv,
    sums, small, tall, halo, ext, local_qkv, cgrad,
    in_sem, own_sem, send_sem, recv_sem,
):
    count = rcv1.shape[0]
    reach = taps.shape[1] - 1
    scale = 1.0 / math.sqrt(count * TILE)
    me = lax.axis_index("ctx")
    barrier = pltpu.get_barrier_semaphore()

    def remote(source, target, sem, peer):
        return pltpu.make_async_remote_copy(
            source, target, send_sem.at[sem], recv_sem.at[sem], device_id={"ctx": peer}, device_id_type=MESH
        )

    def greet(step, carry):
        pl.semaphore_signal(
            barrier, inc=1, device_id={"ctx": lax.rem(me + step, count)}, device_id_type=MESH
        )
        return carry

    loads = [
        pltpu.make_async_copy(source, target, in_sem.at[i])
        for i, (source, target) in enumerate(
            (
                (streams_hbm, st), (filters_hbm, fl), (cot_hbm, ct), (taps_hbm, taps), (e1_hbm, e1),
                (e2_hbm, e2), (e2t_hbm, e2t), (back_hbm, back), (tw_hbm, tw),
            )
        )
    ]
    for load in loads:
        load.start()
    lax.fori_loop(1, count, greet, 0)

    def turn_out(source, target):
        for q in range(source.shape[1] // TILE):
            tile = source[:, q * TILE : (q + 1) * TILE].astype(F32).T
            target[pl.ds(q * TILE // CHANS, TILE // CHANS)] = tile.astype(BF16).reshape(-1, CHANS, TILE)

    loads[0].wait()
    turn_out(st.at[1], snd1.at[:, 0])
    turn_out(st.at[2], snd1.at[:, 1])
    loads[1].wait()
    turn_out(fl, snd1.at[:, 2])
    turn_out(st.at[0], snd2.at[:, 0])
    loads[2].wait()
    turn_out(ct, snd2.at[:, 1])
    for load in loads[3:]:
        load.wait()

    def scatter(source, target, sem):
        own = pltpu.make_async_copy(source.at[me], target.at[me], own_sem.at[sem])
        own.start()

        def send(step, carry):
            peer = lax.rem(me + step, count)
            remote(source.at[peer], target.at[me], sem, peer).start()
            return carry

        lax.fori_loop(1, count, send, 0)
        return own

    def others(source, target, sem):
        return remote(source.at[pl.ds(0, count - 1)], target.at[pl.ds(0, count - 1)], sem, me)

    pl.semaphore_wait(barrier, count - 1)
    own1 = scatter(snd1, rcv1, 0)
    halo_out = remote(st.at[:, pl.ds(TILE - 16, 16)], halo, 6, lax.rem(me + 1, count))
    halo_in = remote(st.at[:, pl.ds(TILE - 16, 16)], halo, 6, me)

    @pl.when(me < count - 1)
    def _():
        halo_out.start()

    own2 = scatter(snd2, rcv2, 1)

    sums[...] = jnp.zeros_like(sums)
    grid[:, pl.ds(0, 8), :] = jnp.zeros((5, 8, TILE), F32)
    ext[:, pl.ds(8, TILE), :] = st[...].astype(F32)

    @pl.when(me > 0)
    def _():
        halo_in.wait_recv()
        ext[:, pl.ds(0, 8), :] = halo[...].astype(F32)[:, 8:, :]

    @pl.when(me == 0)
    def _():
        ext[:, pl.ds(0, 8), :] = jnp.zeros((3, 8, ext.shape[2]), F32)

    for i in range(3):
        for q in range(ext.shape[2] // TILE):
            lanes = pl.ds(q * TILE, TILE)
            total = None
            for j in range(reach + 1):
                term = taps[i, pl.ds(j, 1), lanes] * ext[i, pl.ds(8 - j, TILE), lanes]
                total = term if total is None else total + term
            local_qkv[i, :, lanes] = total

    lane = lax.broadcasted_iota(jnp.int32, (TILE, TILE), 1)

    def unpack(source, index):
        grid[index, pl.ds(8, count * CHANS), :] = source[...].astype(F32).reshape(count * CHANS, TILE)

    def plane(index, c):
        return grid[index, pl.ds(8 + c, count, stride=CHANS), :]

    def convolve(index, c):
        here = plane(index, c)
        before = grid[index, pl.ds(8 - CHANS + c, count, stride=CHANS), :]
        channel = CHANS * me + c
        total = taps_s[index, 0, channel] * here
        for j in range(1, reach + 1):
            moved = pltpu.roll(jnp.where(lane >= TILE - j, before, here), j, 1)
            shifts[index, c, j] = moved
            total = total + taps_s[index, j, channel] * moved
        qkv[index, c] = total
        return total

    def forward(planes, index, h):
        x = jnp.concatenate(planes, 1)
        y = dot(e1[...], jnp.concatenate([x, x], 0))
        re, im = y[:count], y[count:]
        twr, twi = tw[0], tw[1]
        tre, tim = re * twr - im * twi, re * twi + im * twr
        turned = jnp.concatenate(
            [jnp.concatenate([v[:, n * TILE : (n + 1) * TILE] for v in (tre, tim)], 1) for n in range(2)], 0
        )
        high, low = split(turned)
        spec[index, h] = dot(high, e2[0]) + dot(low, e2[0]) + dot(high, e2[1])

    def spectrum(index, h):
        return spec[index, h, :, pl.ds(0, TILE)], spec[index, h, :, pl.ds(TILE, TILE)]

    def inverse(re, im):
        high, low = split(jnp.concatenate([re, im], 1))
        u = dot(high, e2t[0]) + dot(low, e2t[0]) + dot(high, e2t[1])
        ur = jnp.concatenate([u[:count, :TILE], u[count:, :TILE]], 1)
        ui = jnp.concatenate([u[:count, TILE:], u[count:, TILE:]], 1)
        twr, twi = tw[0], tw[1]
        high, low = split(jnp.concatenate([ur * twr + ui * twi, ui * twr - ur * twi], 0))
        return dot(back[0], high) + dot(back[1], high) + dot(back[0], low)

    def put_rows(h, y):
        for n in range(2):
            rows[pl.ds(2 * h + n, count, stride=CHANS), :] = y[:, n * TILE : (n + 1) * TILE]

    def pack(which):
        ret_snd[which] = rows[...].astype(BF16).reshape(count, CHANS, TILE)

    def tap_sums(index, c, grad):
        for j in range(reach + 1):
            moved = plane(index, c) if j == 0 else shifts[index, c, j]
            part = jnp.sum((grad * moved).reshape(count // 8, 8, TILE), 0)
            sums[c * ENTRIES + index * (reach + 1) + j] = part

    own1.wait()
    others(snd1, rcv1, 0).wait_recv()
    for k, index in enumerate((1, 2, 3)):
        unpack(rcv1.at[:, k], index)
    for h in range(2):
        products, kernels = [], []
        for c in (2 * h, 2 * h + 1):
            products.append((convolve(1, c) * convolve(2, c)).astype(BF16))
            kernels.append(plane(3, c).astype(BF16))
        forward(products, 0, h)
        forward(kernels, 1, h)
        pr, pi = spectrum(0, h)
        fr, fi = spectrum(1, h)
        put_rows(h, inverse(pr * fr - pi * fi, pr * fi + pi * fr))
    pack(0)
    own3 = scatter(ret_snd.at[0], ret_rcv.at[0], 2)

    own2.wait()
    others(snd2, rcv2, 1).wait_recv()
    unpack(rcv2.at[:, 0], 0)
    unpack(rcv2.at[:, 1], 4)
    for h in range(2):
        grads = []
        for c in (2 * h, 2 * h + 1):
            upstream = plane(4, c)
            grads.append((upstream * convolve(0, c)).astype(BF16))
            mixed = rows[pl.ds(c, count, stride=CHANS), :].astype(BF16).astype(F32)
            tap_sums(0, c, upstream * mixed)
        forward(grads, 2, h)
    for h in range(2):
        fr, fi = spectrum(1, h)
        gr, gi = spectrum(2, h)
        y = inverse(fr * gr + fi * gi, fr * gi - fi * gr)
        put_rows(h, y)
    pack(1)
    own4 = scatter(ret_snd.at[1], ret_rcv.at[1], 3)
    for c in range(CHANS):
        pgrad = rows[pl.ds(c, count, stride=CHANS), :].astype(BF16).astype(F32)
        tap_sums(1, c, pgrad * qkv[2, c])
        tap_sums(2, c, pgrad * qkv[1, c])
    for h in range(2):
        pr, pi = spectrum(0, h)
        gr, gi = spectrum(2, h)
        put_rows(h, inverse(pr * gr + pi * gi, pr * gi - pi * gr) * scale)
    pack(2)
    own5 = scatter(ret_snd.at[2], ret_rcv.at[2], 4)
    entries = jnp.sum(sums[...], 1)
    row = lax.dot_general(
        jnp.ones((8, TILE), F32), entries, (((1,), (1,)), ((), ())),
        precision=lax.Precision.HIGHEST, preferred_element_type=F32,
    )
    small[...] = row[0:1] * scale
    own6 = pltpu.make_async_copy(small, tall.at[me], own_sem.at[5])
    own6.start()

    def share(step, carry):
        remote(small, tall.at[me], 5, lax.rem(me + step, count)).start()
        return carry

    lax.fori_loop(1, count, share, 0)

    def turn_back(source, q):
        tile = source[pl.ds(q * TILE // CHANS, TILE // CHANS)].astype(F32).reshape(TILE, TILE)
        return tile.T

    strips = [pl.ds(q * TILE, TILE) for q in range(ext.shape[2] // TILE)]
    own3.wait()
    others(ret_snd.at[0], ret_rcv.at[0], 2).wait_recv()
    for q, lanes in enumerate(strips):
        mixed = turn_back(ret_rcv.at[0], q)
        gated_ref[:, lanes] = (local_qkv[0, :, lanes] * mixed).astype(BF16)
        cgrad[0, pl.ds(0, TILE), lanes] = ct[:, lanes].astype(F32) * mixed
    own4.wait()
    others(ret_snd.at[1], ret_rcv.at[1], 3).wait_recv()
    for q, lanes in enumerate(strips):
        pgrad = turn_back(ret_rcv.at[1], q)
        cgrad[1, pl.ds(0, TILE), lanes] = pgrad * local_qkv[2, :, lanes]
        cgrad[2, pl.ds(0, TILE), lanes] = pgrad * local_qkv[1, :, lanes]
    edge = cgrad.at[:, pl.ds(0, 8)]
    beyond = cgrad.at[:, pl.ds(TILE, 8)]
    edge_out = remote(edge, beyond, 7, lax.rem(me + count - 1, count))
    edge_in = remote(edge, beyond, 7, me)

    @pl.when(me > 0)
    def _():
        edge_out.start()

    @pl.when(me < count - 1)
    def _():
        edge_in.wait_recv()

    @pl.when(me == count - 1)
    def _():
        cgrad[:, pl.ds(TILE, 8), :] = jnp.zeros((3, 8, cgrad.shape[2]), F32)

    for i in range(3):
        for lanes in strips:
            total = None
            for j in range(reach + 1):
                term = taps[i, pl.ds(j, 1), lanes] * cgrad[i, pl.ds(j, TILE), lanes]
                total = term if total is None else total + term
            sgrad_ref[i, :, lanes] = total.astype(BF16)
    own5.wait()
    others(ret_snd.at[2], ret_rcv.at[2], 4).wait_recv()
    for q, lanes in enumerate(strips):
        fgrad_ref[:, lanes] = turn_back(ret_rcv.at[2], q).astype(BF16)
    own6.wait()
    others(tall, tall, 5).wait_recv()
    by_entry = tall[...].reshape(count, TILE).T
    width = ext.shape[2]
    total = None
    for c in range(CHANS):
        channel = lax.broadcasted_iota(jnp.int32, (count, width), 1)
        owner = lax.broadcasted_iota(jnp.int32, (count, width), 0)
        place = (channel == CHANS * owner + c).astype(F32)
        term = jnp.dot(
            by_entry[c * ENTRIES : (c + 1) * ENTRIES], place,
            precision=lax.Precision.HIGHEST, preferred_element_type=F32,
        )
        total = term if total is None else total + term
    tgrad_ref[...] = total
    others(snd1, rcv1, 0).wait_send()
    others(snd2, rcv2, 1).wait_send()
    for k in range(3):
        others(ret_snd.at[k], ret_rcv.at[k], 2 + k).wait_send()
    others(tall, tall, 5).wait_send()

    @pl.when(me < count - 1)
    def _():
        halo_out.wait_send()

    @pl.when(me > 0)
    def _():
        edge_out.wait_send()


def local(streams, taps, filters, cotangent):
    rows, width = filters.shape
    count = lax.axis_size("ctx")
    assert rows == TILE and width == CHANS * count and count == TILE
    tables = [jnp.asarray(t) for t in make_tables(count, rows)]
    reach = taps.shape[1] - 1
    any_space = pl.BlockSpec(memory_space=pl.ANY)
    vmem = pl.BlockSpec(memory_space=VMEM)
    line = (count, CHANS, TILE)
    scratch = [
        VMEM(streams.shape, BF16), VMEM(filters.shape, BF16), VMEM(cotangent.shape, BF16), VMEM(taps.shape, F32),
        *[VMEM(t.shape, t.dtype) for t in tables],
        VMEM((count, 3, CHANS, TILE), BF16), VMEM((count, 2, CHANS, TILE), BF16),
        VMEM((count, 3, CHANS, TILE), BF16), VMEM((count, 2, CHANS, TILE), BF16),
        VMEM((5, 8 + count * CHANS, TILE), F32),
        VMEM((3, CHANS, reach + 1, count, TILE), F32),
        VMEM((3, CHANS, count, TILE), F32),
        VMEM((3, 2, 2 * count, 2 * TILE), F32),
        VMEM((count * CHANS, TILE), F32),
        VMEM((3,) + line, BF16), VMEM((3,) + line, BF16),
        VMEM((TILE, 8, TILE), F32), VMEM((1, TILE), F32), VMEM((count, 1, TILE), F32),
        VMEM((3, 16, width), BF16),
        VMEM((3, 8 + TILE, width), F32),
        VMEM((3, TILE, width), F32),
        VMEM((3, TILE + 8, width), F32),
        pltpu.SemaphoreType.DMA((9,)), pltpu.SemaphoreType.DMA((6,)),
        pltpu.SemaphoreType.DMA((8,)), pltpu.SemaphoreType.DMA((8,)),
    ]
    gated, sgrad, fgrad, tgrad = pl.pallas_call(
        block_kernel,
        out_shape=[
            jax.ShapeDtypeStruct(cotangent.shape, BF16),
            jax.ShapeDtypeStruct(streams.shape, BF16),
            jax.ShapeDtypeStruct(filters.shape, BF16),
            jax.ShapeDtypeStruct((ENTRIES, width), F32),
        ],
        in_specs=[any_space] * 9 + [pl.BlockSpec(memory_space=pltpu.SMEM)],
        out_specs=[vmem] * 4,
        scratch_shapes=scratch,
        compiler_params=pltpu.CompilerParams(collective_id=0, has_side_effects=True),
    )(streams, filters, cotangent, taps, *tables, taps)
    return gated, sgrad, fgrad, tgrad[: taps.shape[0] * taps.shape[1]].reshape(taps.shape)


def solution(mesh):
    in_specs = (P(None, "ctx", "fft"), P(None, None, "fft"), P("ctx", "fft"), P("ctx", "fft"))
    out_specs = (P("ctx", "fft"), P(None, "ctx", "fft"), P("ctx", "fft"), P(None, None, "fft"))
    return jax.shard_map(local, mesh=mesh, in_specs=in_specs, out_specs=out_specs, check_vma=False)
```

time: 111 us -> 63.4 us (0.57)
  other arithmetic: 14.2 us -> 0 us
  local copies, waits for them, and re-layouts: 17.7 us -> 5.45 us
  Pallas kernels: 67.7 us -> 57 us
  matrix products: 9.52 us -> 0 us
    pallas_call x2 -> x1, Pallas kernels: 67.7 us -> 57 us  [local(): pl.pallas_call(block_kernel, out_shape=[jax.ShapeDtypeStruct(cotangent.sh...]
    dot_general x12 -> x0, matrix products: 9.52 us -> none  [the longest x3 2.99 us: forward(): z = dot('ckb,bq->ckq', turned, jnp.asarray(e2))]
    unnamed x48 -> x5, local copies, waits for them, and re-layouts: 8.36 us -> 4.03 us
    add x4 -> x0, other arithmetic: 3.57 us -> none  [the longest x1 2.52 us: owner_math(): sum((taps[:, j, :, None] * shifts[j] for j in range(reach + 1)))]
    reduce_sum x2 -> x0, other arithmetic: 3.36 us -> none  [owner_math(): jnp.sum(cgrad * shifts[j], axis=-1)]
    reshape x2 -> x0, other arithmetic: 2.57 us -> none  [the longest x1 2.52 us: owner_math(): return (gated, sgrad.reshape((3,) + grid), fgrad, tgrad)]
    reshape x4 -> x1, local copies, waits for them, and re-layouts: 3.61 us -> 1.42 us  [local(): tgrad[:taps.shape[0] * taps.shape[1]].reshape(taps.shape)]
    slice x3 -> x0, local copies, waits for them, and re-layouts: 2.02 us -> none  [the longest x1 1.06 us: owner_math(): taps[:, j, :, None] * shifts[j]]
where the time goes in v2:
time: 63.4 us; the launch traced here: 63.1 us
  Pallas kernels  57 us (90%)
  local copies, waits for them, and re-layouts  5.45 us (9%)
  between operations  0.64 us (1%)
    pallas_call x1, Pallas kernels, local(): pl.pallas_call(block_kernel, out_shape=[jax.ShapeDtypeStruct(cotangent.sh...  57 us
    unnamed x5, local copies, waits for them, and re-layouts  4.03 us
    reshape x1, local copies, waits for them, and re-layouts, local(): tgrad[:taps.shape[0] * taps.shape[1]].reshape(taps.shape)  1.42 us

profile of v2, /device:TPU:6, one launch (start us, length us, event | category | flops | bytes accessed | tf_op | source)
XLA Modules:
  0.0 63.1 jit_solution(17600875275855542246)
XLA Ops:
  0.6 57.0 %shard_map.120 = (bf16[128,512]{1,0:T(8,128)(2,1)}, bf16[3,128,512]{2,1,0:T(8,128)(2,1)}, bf16[128,512]{1,0:T(8,128)(2,1)}, f32[24,512]{1,0:T(8,128)}) custom-call(bf16[3,128,512]{2,1,0:T(8,128)(2,1)} %streams_hbm.1, bf16[128,512]{1,0:T(8,128)(2,1)} %filters_hbm.1, bf16[128,512]{1,0:T(8,128)(2,1)} %cot_hbm.1, f32[3,7,512]{2,1,0:T(8,128)} %taps_s.1, ...), custom_call_target="tpu_custom_call" | custom-call | tf_op jit(solution)/shard_map/pallas_call | solution.py:372
  57.7 1.4 %reshape.11 = f32[3,7,512]{2,1,0:T(8,128)} reshape(f32[21,512]{1,0:T(8,128)} %bitcast.1) | data formatting | bytes 86016 | tf_op jit(solution)/shard_map/reshape | solution.py:385
  59.1 1.6 %copy.16 = bf16[128,512]{1,0:T(8,128)(2,1)} copy(bf16[128,512]{1,0:T(8,128)(2,1)} %get-tuple-element.16) | data formatting | bytes 262144
  60.7 0.0 copy-start
  60.7 1.8 %copy.17 = bf16[3,128,512]{2,1,0:T(8,128)(2,1)} copy(bf16[3,128,512]{2,1,0:T(8,128)(2,1)} %get-tuple-element.17) | data formatting | bytes 786432
  62.5 0.0 copy-done
  62.5 0.7 %copy.18 = bf16[128,512]{1,0:T(8,128)(2,1)} copy(bf16[128,512]{1,0:T(8,128)(2,1)S(1)} %copy-done) | data formatting | bytes 262144
Async XLA Ops:
  60.7 1.8 %copy-start = (bf16[128,512]{1,0:T(8,128)(2,1)S(1)}, bf16[128,512]{1,0:T(8,128)(2,1)}, u32[]{:S(2)}) copy-start(bf16[128,512]{1,0:T(8,128)(2,1)} %get-tuple-element.18) | copy-start | bytes 393220

commit v3 on v2

--- a/solution.py
+++ b/solution.py
@@ -15,6 +15,8 @@
 CHANS = 4
 TILE = 128
 ENTRIES = 24
+UNROLL = 7
+LATER = (1, 8, 9)
 
 
 def halves(table):
@@ -46,15 +48,21 @@
     return high, (x - high.astype(F32)).astype(BF16)
 
 
+def turn_back(source, q):
+    tile = source[pl.ds(q * TILE // CHANS, TILE // CHANS)].astype(F32).reshape(TILE, TILE)
+    return tile.T
+
+
 def block_kernel(
-    streams_hbm, filters_hbm, cot_hbm, taps_hbm, e1_hbm, e2_hbm, e2t_hbm, back_hbm, tw_hbm, taps_s,
-    gated_ref, sgrad_ref, fgrad_ref, tgrad_ref,
+    streams_hbm, filters_hbm, cot_hbm, taps_hbm, e1_hbm, e2_hbm, e2t_hbm, back_hbm, tw_hbm,
+    gated_ref, sgrad_ref, fgrad_raw, tall,
     st, fl, ct, taps, e1, e2, e2t, back, tw,
-    snd1, snd2, rcv1, rcv2, grid, shifts, qkv, spec, rows, ret_snd, ret_rcv,
-    sums, small, tall, halo, ext, local_qkv, cgrad,
+    snd1, snd2, rcv1, rcv2, own_taps, grid, shifts, qkv, spec, rows, mixed_rows, ret_snd, ret_rcv,
+    sums, small, halo, ext, local_qkv, cgrad,
     in_sem, own_sem, send_sem, recv_sem,
 ):
     count = rcv1.shape[0]
+    width = ext.shape[2]
     reach = taps.shape[1] - 1
     scale = 1.0 / math.sqrt(count * TILE)
     me = lax.axis_index("ctx")
@@ -65,11 +73,17 @@
             source, target, send_sem.at[sem], recv_sem.at[sem], device_id={"ctx": peer}, device_id_type=MESH
         )
 
-    def greet(step, carry):
-        pl.semaphore_signal(
-            barrier, inc=1, device_id={"ctx": lax.rem(me + step, count)}, device_id_type=MESH
-        )
-        return carry
+    def each_peer(visit):
+        def several(block, carry):
+            for k in range(UNROLL):
+                visit(lax.rem(me + 1 + UNROLL * block + k, count))
+            return carry
+
+        blocks = (count - 1) // UNROLL
+        lax.fori_loop(0, blocks, several, 0)
+        for step in range(1 + UNROLL * blocks, count):
+            visit(lax.rem(me + step, count))
+
 
     loads = [
         pltpu.make_async_copy(source, target, in_sem.at[i])
@@ -82,7 +96,11 @@
     ]
     for load in loads:
         load.start()
-    lax.fori_loop(1, count, greet, 0)
+
+    def greet(peer):
+        pl.semaphore_signal(barrier, inc=1, device_id={"ctx": peer}, device_id_type=MESH)
+
+    each_peer(greet)
 
     def turn_out(source, target):
         for q in range(source.shape[1] // TILE):
@@ -93,30 +111,28 @@
     turn_out(st.at[1], snd1.at[:, 0])
     turn_out(st.at[2], snd1.at[:, 1])
     loads[1].wait()
-    turn_out(fl, snd1.at[:, 2])
-    turn_out(st.at[0], snd2.at[:, 0])
+    turn_out(fl, snd2.at[0])
+    turn_out(st.at[0], snd2.at[1])
     loads[2].wait()
-    turn_out(ct, snd2.at[:, 1])
+    turn_out(ct, snd2.at[2])
     for load in loads[3:]:
         load.wait()
+    for i in range(3):
+        for c in range(CHANS):
+            chosen = lax.broadcasted_iota(jnp.int32, (reach + 1, width), 1) == CHANS * me + c
+            tap = jnp.sum(jnp.where(chosen, taps[i], 0.0), 1, keepdims=True)
+            own_taps[c, i, pl.ds(0, reach + 1), :] = jnp.broadcast_to(tap, (reach + 1, TILE))
 
     def scatter(source, target, sem):
         own = pltpu.make_async_copy(source.at[me], target.at[me], own_sem.at[sem])
         own.start()
-
-        def send(step, carry):
-            peer = lax.rem(me + step, count)
-            remote(source.at[peer], target.at[me], sem, peer).start()
-            return carry
-
-        lax.fori_loop(1, count, send, 0)
+        each_peer(lambda peer: remote(source.at[peer], target.at[me], sem, peer).start())
         return own
 
     def others(source, target, sem):
         return remote(source.at[pl.ds(0, count - 1)], target.at[pl.ds(0, count - 1)], sem, me)
 
     pl.semaphore_wait(barrier, count - 1)
-    own1 = scatter(snd1, rcv1, 0)
     halo_out = remote(st.at[:, pl.ds(TILE - 16, 16)], halo, 6, lax.rem(me + 1, count))
     halo_in = remote(st.at[:, pl.ds(TILE - 16, 16)], halo, 6, me)
 
@@ -124,7 +140,8 @@
     def _():
         halo_out.start()
 
-    own2 = scatter(snd2, rcv2, 1)
+    own1 = scatter(snd1, rcv1, 0)
+    own2 = [scatter(snd2.at[k], rcv2.at[k], sem) for k, sem in enumerate(LATER)]
 
     sums[...] = jnp.zeros_like(sums)
     grid[:, pl.ds(0, 8), :] = jnp.zeros((5, 8, TILE), F32)
@@ -159,12 +176,11 @@
     def convolve(index, c):
         here = plane(index, c)
         before = grid[index, pl.ds(8 - CHANS + c, count, stride=CHANS), :]
-        channel = CHANS * me + c
-        total = taps_s[index, 0, channel] * here
+        total = own_taps[c, index, pl.ds(0, 1), :] * here
         for j in range(1, reach + 1):
             moved = pltpu.roll(jnp.where(lane >= TILE - j, before, here), j, 1)
             shifts[index, c, j] = moved
-            total = total + taps_s[index, j, channel] * moved
+            total = total + own_taps[c, index, pl.ds(j, 1), :] * moved
         qkv[index, c] = total
         return total
 
@@ -207,33 +223,33 @@
 
     own1.wait()
     others(snd1, rcv1, 0).wait_recv()
-    for k, index in enumerate((1, 2, 3)):
-        unpack(rcv1.at[:, k], index)
+    unpack(rcv1.at[:, 0], 1)
+    unpack(rcv1.at[:, 1], 2)
     for h in range(2):
-        products, kernels = [], []
-        for c in (2 * h, 2 * h + 1):
-            products.append((convolve(1, c) * convolve(2, c)).astype(BF16))
-            kernels.append(plane(3, c).astype(BF16))
+        products = [(convolve(1, c) * convolve(2, c)).astype(BF16) for c in (2 * h, 2 * h + 1)]
         forward(products, 0, h)
-        forward(kernels, 1, h)
+    own2[0].wait()
+    others(snd2.at[0], rcv2.at[0], LATER[0]).wait_recv()
+    unpack(rcv2.at[0], 3)
+    for h in range(2):
+        forward([plane(3, c).astype(BF16) for c in (2 * h, 2 * h + 1)], 1, h)
         pr, pi = spectrum(0, h)
         fr, fi = spectrum(1, h)
         put_rows(h, inverse(pr * fr - pi * fi, pr * fi + pi * fr))
     pack(0)
     own3 = scatter(ret_snd.at[0], ret_rcv.at[0], 2)
 
-    own2.wait()
-    others(snd2, rcv2, 1).wait_recv()
-    unpack(rcv2.at[:, 0], 0)
-    unpack(rcv2.at[:, 1], 4)
+    own2[1].wait()
+    others(snd2.at[1], rcv2.at[1], LATER[1]).wait_recv()
+    unpack(rcv2.at[1], 0)
+    for c in range(CHANS):
+        convolve(0, c)
+        mixed_rows[c] = rows[pl.ds(c, count, stride=CHANS), :].astype(BF16).astype(F32)
+    own2[2].wait()
+    others(snd2.at[2], rcv2.at[2], LATER[2]).wait_recv()
+    unpack(rcv2.at[2], 4)
     for h in range(2):
-        grads = []
-        for c in (2 * h, 2 * h + 1):
-            upstream = plane(4, c)
-            grads.append((upstream * convolve(0, c)).astype(BF16))
-            mixed = rows[pl.ds(c, count, stride=CHANS), :].astype(BF16).astype(F32)
-            tap_sums(0, c, upstream * mixed)
-        forward(grads, 2, h)
+        forward([(plane(4, c) * qkv[0, c]).astype(BF16) for c in (2 * h, 2 * h + 1)], 2, h)
     for h in range(2):
         fr, fi = spectrum(1, h)
         gr, gi = spectrum(2, h)
@@ -242,33 +258,31 @@
     pack(1)
     own4 = scatter(ret_snd.at[1], ret_rcv.at[1], 3)
     for c in range(CHANS):
+        tap_sums(0, c, plane(4, c) * mixed_rows[c])
         pgrad = rows[pl.ds(c, count, stride=CHANS), :].astype(BF16).astype(F32)
         tap_sums(1, c, pgrad * qkv[2, c])
         tap_sums(2, c, pgrad * qkv[1, c])
-    for h in range(2):
-        pr, pi = spectrum(0, h)
-        gr, gi = spectrum(2, h)
-        put_rows(h, inverse(pr * gr + pi * gi, pr * gi - pi * gr) * scale)
-    pack(2)
-    own5 = scatter(ret_snd.at[2], ret_rcv.at[2], 4)
     entries = jnp.sum(sums[...], 1)
     row = lax.dot_general(
         jnp.ones((8, TILE), F32), entries, (((1,), (1,)), ((), ())),
         precision=lax.Precision.HIGHEST, preferred_element_type=F32,
     )
     small[...] = row[0:1] * scale
+    for h in range(2):
+        pr, pi = spectrum(0, h)
+        gr, gi = spectrum(2, h)
+        put_rows(h, inverse(pr * gr + pi * gi, pr * gi - pi * gr) * scale)
+    pack(2)
+    own5 = pltpu.make_async_copy(ret_snd.at[2].at[me], fgrad_raw.at[me], own_sem.at[4])
+    own5.start()
     own6 = pltpu.make_async_copy(small, tall.at[me], own_sem.at[5])
     own6.start()
 
-    def share(step, carry):
-        remote(small, tall.at[me], 5, lax.rem(me + step, count)).start()
-        return carry
-
-    lax.fori_loop(1, count, share, 0)
-
-    def turn_back(source, q):
-        tile = source[pl.ds(q * TILE // CHANS, TILE // CHANS)].astype(F32).reshape(TILE, TILE)
-        return tile.T
+    def last(peer):
+        remote(ret_snd.at[2].at[peer], fgrad_raw.at[me], 4, peer).start()
+        remote(small, tall.at[me], 5, peer).start()
+
+    each_peer(last)
 
     strips = [pl.ds(q * TILE, TILE) for q in range(ext.shape[2] // TILE)]
     own3.wait()
@@ -292,53 +306,74 @@
     def _():
         edge_out.start()
 
+    def correlate(first, number):
+        for i in range(3):
+            for lanes in strips:
+                total = None
+                for j in range(reach + 1):
+                    term = taps[i, pl.ds(j, 1), lanes] * cgrad[i, pl.ds(first + j, number), lanes]
+                    total = term if total is None else total + term
+                sgrad_ref[i, pl.ds(first, number), lanes] = total.astype(BF16)
+
+    correlate(0, TILE - 16)
+
     @pl.when(me < count - 1)
     def _():
         edge_in.wait_recv()
 
     @pl.when(me == count - 1)
     def _():
-        cgrad[:, pl.ds(TILE, 8), :] = jnp.zeros((3, 8, cgrad.shape[2]), F32)
-
-    for i in range(3):
-        for lanes in strips:
-            total = None
-            for j in range(reach + 1):
-                term = taps[i, pl.ds(j, 1), lanes] * cgrad[i, pl.ds(j, TILE), lanes]
-                total = term if total is None else total + term
-            sgrad_ref[i, :, lanes] = total.astype(BF16)
+        cgrad[:, pl.ds(TILE, 8), :] = jnp.zeros((3, 8, width), F32)
+
+    correlate(TILE - 16, 16)
     own5.wait()
-    others(ret_snd.at[2], ret_rcv.at[2], 4).wait_recv()
-    for q, lanes in enumerate(strips):
-        fgrad_ref[:, lanes] = turn_back(ret_rcv.at[2], q).astype(BF16)
+    others(ret_snd.at[2], fgrad_raw, 4).wait_recv()
     own6.wait()
     others(tall, tall, 5).wait_recv()
-    by_entry = tall[...].reshape(count, TILE).T
-    width = ext.shape[2]
-    total = None
+    others(snd1, rcv1, 0).wait_send()
+    for k, sem in enumerate(LATER):
+        others(snd2.at[k], rcv2.at[k], sem).wait_send()
+    for k in range(2):
+        others(ret_snd.at[k], ret_rcv.at[k], 2 + k).wait_send()
+    others(ret_snd.at[2], fgrad_raw, 4).wait_send()
+    others(tall, tall, 5).wait_send()
+
+    @pl.when(me < count - 1)
+    def _():
+        halo_out.wait_send()
+
+    @pl.when(me > 0)
+    def _():
+        edge_out.wait_send()
+
+
+def result_kernel(
+    gated, sgrad, fgrad_raw, tall, gated_hbm, sgrad_hbm, fgrad_hbm, tgrad_hbm, fgrad, tgrad, spread, sem
+):
+    count = tall.shape[0]
+    terms = tgrad.shape[1]
+    stores = [
+        pltpu.make_async_copy(source, target, sem.at[i])
+        for i, (source, target) in enumerate(
+            ((gated, gated_hbm), (sgrad, sgrad_hbm), (fgrad, fgrad_hbm), (tgrad, tgrad_hbm))
+        )
+    ]
+    stores[0].start()
+    stores[1].start()
+    for q in range(fgrad.shape[1] // TILE):
+        fgrad[:, q * TILE : (q + 1) * TILE] = turn_back(fgrad_raw, q).astype(BF16)
+    stores[2].start()
+    entries = tall[...].reshape(count, TILE)
     for c in range(CHANS):
-        channel = lax.broadcasted_iota(jnp.int32, (count, width), 1)
-        owner = lax.broadcasted_iota(jnp.int32, (count, width), 0)
-        place = (channel == CHANS * owner + c).astype(F32)
-        term = jnp.dot(
-            by_entry[c * ENTRIES : (c + 1) * ENTRIES], place,
-            precision=lax.Precision.HIGHEST, preferred_element_type=F32,
-        )
-        total = term if total is None else total + term
-    tgrad_ref[...] = total
-    others(snd1, rcv1, 0).wait_send()
-    others(snd2, rcv2, 1).wait_send()
-    for k in range(3):
-        others(ret_snd.at[k], ret_rcv.at[k], 2 + k).wait_send()
-    others(tall, tall, 5).wait_send()
-
-    @pl.when(me < count - 1)
-    def _():
-        halo_out.wait_send()
-
-    @pl.when(me > 0)
-    def _():
-        edge_out.wait_send()
+        moved = pltpu.roll(entries, TILE - c * ENTRIES, 1) if c else entries
+        spread[pl.ds(c, count, stride=CHANS), :] = moved
+    for q in range(fgrad.shape[1] // TILE):
+        by_entry = spread[q * TILE : (q + 1) * TILE, :].T
+        for i in range(tgrad.shape[0]):
+            tgrad[i, :, q * TILE : (q + 1) * TILE] = by_entry[i * terms : (i + 1) * terms]
+    stores[3].start()
+    for store in stores:
+        store.wait()
 
 
 def local(streams, taps, filters, cotangent):
@@ -347,42 +382,60 @@
     assert rows == TILE and width == CHANS * count and count == TILE
     tables = [jnp.asarray(t) for t in make_tables(count, rows)]
     reach = taps.shape[1] - 1
-    any_space = pl.BlockSpec(memory_space=pl.ANY)
+    hbm = pl.BlockSpec(memory_space=pltpu.HBM)
     vmem = pl.BlockSpec(memory_space=VMEM)
     line = (count, CHANS, TILE)
+    pair = (count, 2, CHANS, TILE)
     scratch = [
         VMEM(streams.shape, BF16), VMEM(filters.shape, BF16), VMEM(cotangent.shape, BF16), VMEM(taps.shape, F32),
         *[VMEM(t.shape, t.dtype) for t in tables],
-        VMEM((count, 3, CHANS, TILE), BF16), VMEM((count, 2, CHANS, TILE), BF16),
-        VMEM((count, 3, CHANS, TILE), BF16), VMEM((count, 2, CHANS, TILE), BF16),
+        VMEM(pair, BF16), VMEM((3,) + line, BF16), VMEM(pair, BF16), VMEM((3,) + line, BF16),
+        VMEM((CHANS, 3, 8, TILE), F32),
         VMEM((5, 8 + count * CHANS, TILE), F32),
         VMEM((3, CHANS, reach + 1, count, TILE), F32),
         VMEM((3, CHANS, count, TILE), F32),
         VMEM((3, 2, 2 * count, 2 * TILE), F32),
-        VMEM((count * CHANS, TILE), F32),
-        VMEM((3,) + line, BF16), VMEM((3,) + line, BF16),
-        VMEM((TILE, 8, TILE), F32), VMEM((1, TILE), F32), VMEM((count, 1, TILE), F32),
+        VMEM((count * CHANS, TILE), F32), VMEM((CHANS, count, TILE), F32),
+        VMEM((3,) + line, BF16), VMEM((2,) + line, BF16),
+        VMEM((TILE, 8, TILE), F32), VMEM((1, TILE), F32),
         VMEM((3, 16, width), BF16),
         VMEM((3, 8 + TILE, width), F32),
         VMEM((3, TILE, width), F32),
         VMEM((3, TILE + 8, width), F32),
-        pltpu.SemaphoreType.DMA((9,)), pltpu.SemaphoreType.DMA((6,)),
-        pltpu.SemaphoreType.DMA((8,)), pltpu.SemaphoreType.DMA((8,)),
+        pltpu.SemaphoreType.DMA((9,)), pltpu.SemaphoreType.DMA((10,)),
+        pltpu.SemaphoreType.DMA((10,)), pltpu.SemaphoreType.DMA((10,)),
     ]
-    gated, sgrad, fgrad, tgrad = pl.pallas_call(
+    parts = pl.pallas_call(
         block_kernel,
         out_shape=[
             jax.ShapeDtypeStruct(cotangent.shape, BF16),
             jax.ShapeDtypeStruct(streams.shape, BF16),
-            jax.ShapeDtypeStruct(filters.shape, BF16),
-            jax.ShapeDtypeStruct((ENTRIES, width), F32),
+            jax.ShapeDtypeStruct(line, BF16),
+            jax.ShapeDtypeStruct((count, 1, TILE), F32),
         ],
-        in_specs=[any_space] * 9 + [pl.BlockSpec(memory_space=pltpu.SMEM)],
+        in_specs=[hbm] * 9,
         out_specs=[vmem] * 4,
         scratch_shapes=scratch,
-        compiler_params=pltpu.CompilerParams(collective_id=0, has_side_effects=True),
-    )(streams, filters, cotangent, taps, *tables, taps)
-    return gated, sgrad, fgrad, tgrad[: taps.shape[0] * taps.shape[1]].reshape(taps.shape)
+        compiler_params=pltpu.CompilerParams(
+            collective_id=0, has_side_effects=True, vmem_limit_bytes=40 << 20
+        ),
+    )(*[pltpu.with_memory_space_constraint(x, pltpu.HBM) for x in (streams, filters, cotangent, taps, *tables)])
+    return pl.pallas_call(
+        result_kernel,
+        out_shape=[
+            jax.ShapeDtypeStruct(cotangent.shape, BF16),
+            jax.ShapeDtypeStruct(streams.shape, BF16),
+            jax.ShapeDtypeStruct(filters.shape, BF16),
+            jax.ShapeDtypeStruct(taps.shape, F32),
+        ],
+        in_specs=[vmem] * 4,
+        out_specs=[hbm] * 4,
+        scratch_shapes=[
+            VMEM(filters.shape, BF16), VMEM(taps.shape, F32), VMEM((count * CHANS, TILE), F32),
+            pltpu.SemaphoreType.DMA((4,)),
+        ],
+        compiler_params=pltpu.CompilerParams(vmem_limit_bytes=8 << 20),
+    )(*parts)
 
 
 def solution(mesh):

time: 63.4 us -> 54.5 us (0.86)
  local copies, waits for them, and re-layouts: 5.45 us -> 0 us
  Pallas kernels: 57 us -> 53.7 us
    pallas_call x1, Pallas kernels: 57 us -> 52.8 us  [local(): pl.pallas_call(block_kernel, out_shape=[jax.ShapeDtypeStruct(cotangent.sh...]
    unnamed x5 -> x0, local copies, waits for them, and re-layouts: 4.03 us -> none
    reshape x1 -> x0, local copies, waits for them, and re-layouts: 1.42 us -> none  [local(): tgrad[:taps.shape[0] * taps.shape[1]].reshape(taps.shape)]
    pallas_call x0 -> x1, Pallas kernels: none -> 0.9 us  [local(): pl.pallas_call(result_kernel, out_shape=[jax.ShapeDtypeStruct(cotangent.s...]
where the time goes in v3:
time: 54.5 us; the launch traced here: 54.4 us
  Pallas kernels  53.7 us (99%)
  between operations  0.64 us (1%)
    pallas_call x1, Pallas kernels, local(): pl.pallas_call(block_kernel, out_shape=[jax.ShapeDtypeStruct(cotangent.sh...  52.8 us

profile of v3, /device:TPU:6, one launch (start us, length us, event | category | flops | bytes accessed | tf_op | source)
XLA Modules:
  0.0 54.4 jit_solution(15796461806373487752)
XLA Ops:
  0.6 52.8 %shard_map.120 = (bf16[128,512]{1,0:T(8,128)(2,1)S(1)}, bf16[3,128,512]{2,1,0:T(8,128)(2,1)S(1)}, bf16[128,4,128]{2,1,0:T(4,128)(2,1)S(1)}, f32[128,1,128]{2,1,0:T(1,128)S(1)}) custom-call(bf16[3,128,512]{2,1,0:T(8,128)(2,1)} %streams_hbm.1, bf16[128,512]{1,0:T(8,128)(2,1)} %filters_hbm.1, bf16[128,512]{1,0:T(8,128)(2,1)} %cot_hbm.1, f32[3,7,512]{2,1,0:T(8,128)} %taps_hbm.1, ...), custom_call_target="tpu_custom_call" | custom-call | tf_op jit(solution)/shard_map/pallas_call | solution.py:408
  53.5 0.9 %shard_map.121 = (bf16[128,512]{1,0:T(8,128)(2,1)}, bf16[3,128,512]{2,1,0:T(8,128)(2,1)}, bf16[128,512]{1,0:T(8,128)(2,1)}, f32[3,7,512]{2,1,0:T(8,128)}) custom-call(bf16[128,512]{1,0:T(8,128)(2,1)S(1)} %get-tuple-element.8.gated, bf16[3,128,512]{2,1,0:T(8,128)(2,1)S(1)} %get-tuple-element.9.sgrad, bf16[128,4,128]{2,1,0:T(4,128)(2,1)S(1)} %get-tuple-element.10.fgrad_raw, ...), custom_call_target="tpu_custom_call" | custom-call | tf_op jit(solution)/shard_map/pallas_call | solution.py:423

commit v4 on v3

--- a/solution.py
+++ b/solution.py
@@ -15,7 +15,7 @@
 CHANS = 4
 TILE = 128
 ENTRIES = 24
-UNROLL = 7
+Y_SIZE, Z_SIZE, X_SIZE = 8, 8, 2
 LATER = (1, 8, 9)
 
 
@@ -55,7 +55,7 @@
 
 def block_kernel(
     streams_hbm, filters_hbm, cot_hbm, taps_hbm, e1_hbm, e2_hbm, e2t_hbm, back_hbm, tw_hbm,
-    gated_ref, sgrad_ref, fgrad_raw, tall,
+    gated_ref, sgrad_ref, fgrad_ref, tall,
     st, fl, ct, taps, e1, e2, e2t, back, tw,
     snd1, snd2, rcv1, rcv2, own_taps, grid, shifts, qkv, spec, rows, mixed_rows, ret_snd, ret_rcv,
     sums, small, halo, ext, local_qkv, cgrad,
@@ -73,17 +73,27 @@
             source, target, send_sem.at[sem], recv_sem.at[sem], device_id={"ctx": peer}, device_id_type=MESH
         )
 
+    zx_count = Z_SIZE * X_SIZE
+    y, zx = me // zx_count, lax.rem(me, zx_count)
+    z, x = zx // X_SIZE, lax.rem(zx, X_SIZE)
+    planes = [
+        lax.rem(z + dz, Z_SIZE) * X_SIZE + lax.rem(x + dx, X_SIZE)
+        for dz in (4, 3, 5, 2, 6, 1, 7, 0)
+        for dx in (1, 0)
+    ]
+
     def each_peer(visit):
-        def several(block, carry):
-            for k in range(UNROLL):
-                visit(lax.rem(me + 1 + UNROLL * block + k, count))
+        def row(step, carry):
+            half = (step + 1) // 2
+            dy = 4 + half - 2 * half * lax.rem(step, 2)
+            base = lax.rem(y + dy, Y_SIZE) * zx_count
+            for plane_at in planes:
+                visit(base + plane_at)
             return carry
 
-        blocks = (count - 1) // UNROLL
-        lax.fori_loop(0, blocks, several, 0)
-        for step in range(1 + UNROLL * blocks, count):
-            visit(lax.rem(me + step, count))
-
+        lax.fori_loop(0, Y_SIZE - 1, row, 0)
+        for plane_at in planes[:-1]:
+            visit(y * zx_count + plane_at)
 
     loads = [
         pltpu.make_async_copy(source, target, in_sem.at[i])
@@ -112,9 +122,19 @@
     turn_out(st.at[2], snd1.at[:, 1])
     loads[1].wait()
     turn_out(fl, snd2.at[0])
-    turn_out(st.at[0], snd2.at[1])
     loads[2].wait()
-    turn_out(ct, snd2.at[2])
+    lane = lax.broadcasted_iota(jnp.int32, (TILE, TILE), 1)
+    low = lax.rem(lane, CHANS) < 2
+    for q in range(width // TILE):
+        lanes = pl.ds(q * TILE, TILE)
+        place = pl.ds(q * TILE // CHANS, TILE // CHANS)
+        first, second = st[0, :, lanes].astype(F32), ct[:, lanes].astype(F32)
+        tiles = (
+            jnp.where(low, first, pltpu.roll(second, 2, 1)),
+            jnp.where(low, pltpu.roll(first, TILE - 2, 1), second),
+        )
+        for h, tile in enumerate(tiles):
+            snd2.at[1 + h][place] = tile.T.astype(BF16).reshape(-1, CHANS, TILE)
     for load in loads[3:]:
         load.wait()
     for i in range(3):
@@ -165,17 +185,22 @@
                 total = term if total is None else total + term
             local_qkv[i, :, lanes] = total
 
-    lane = lax.broadcasted_iota(jnp.int32, (TILE, TILE), 1)
+    def slot(index, c):
+        if index in (1, 2, 3):
+            return index, c
+        return (0, 4)[c // 2], c % 2 + (2 if index == 4 else 0)
 
     def unpack(source, index):
         grid[index, pl.ds(8, count * CHANS), :] = source[...].astype(F32).reshape(count * CHANS, TILE)
 
     def plane(index, c):
-        return grid[index, pl.ds(8 + c, count, stride=CHANS), :]
+        block, line = slot(index, c)
+        return grid[block, pl.ds(8 + line, count, stride=CHANS), :]
 
     def convolve(index, c):
         here = plane(index, c)
-        before = grid[index, pl.ds(8 - CHANS + c, count, stride=CHANS), :]
+        block, line = slot(index, c)
+        before = grid[block, pl.ds(8 - CHANS + line, count, stride=CHANS), :]
         total = own_taps[c, index, pl.ds(0, 1), :] * here
         for j in range(1, reach + 1):
             moved = pltpu.roll(jnp.where(lane >= TILE - j, before, here), j, 1)
@@ -208,9 +233,9 @@
         high, low = split(jnp.concatenate([ur * twr + ui * twi, ui * twr - ur * twi], 0))
         return dot(back[0], high) + dot(back[1], high) + dot(back[0], low)
 
-    def put_rows(h, y):
+    def put_rows(h, values):
         for n in range(2):
-            rows[pl.ds(2 * h + n, count, stride=CHANS), :] = y[:, n * TILE : (n + 1) * TILE]
+            rows[pl.ds(2 * h + n, count, stride=CHANS), :] = values[:, n * TILE : (n + 1) * TILE]
 
     def pack(which):
         ret_snd[which] = rows[...].astype(BF16).reshape(count, CHANS, TILE)
@@ -239,103 +264,99 @@
     pack(0)
     own3 = scatter(ret_snd.at[0], ret_rcv.at[0], 2)
 
-    own2[1].wait()
-    others(snd2.at[1], rcv2.at[1], LATER[1]).wait_recv()
-    unpack(rcv2.at[1], 0)
     for c in range(CHANS):
-        convolve(0, c)
         mixed_rows[c] = rows[pl.ds(c, count, stride=CHANS), :].astype(BF16).astype(F32)
-    own2[2].wait()
-    others(snd2.at[2], rcv2.at[2], LATER[2]).wait_recv()
-    unpack(rcv2.at[2], 4)
+    own4 = []
     for h in range(2):
-        forward([(plane(4, c) * qkv[0, c]).astype(BF16) for c in (2 * h, 2 * h + 1)], 2, h)
-    for h in range(2):
+        pair = (2 * h, 2 * h + 1)
+        own2[1 + h].wait()
+        others(snd2.at[1 + h], rcv2.at[1 + h], LATER[1 + h]).wait_recv()
+        unpack(rcv2.at[1 + h], (0, 4)[h])
+        forward([(plane(4, c) * convolve(0, c)).astype(BF16) for c in pair], 2, h)
+        pr, pi = spectrum(0, h)
         fr, fi = spectrum(1, h)
         gr, gi = spectrum(2, h)
-        y = inverse(fr * gr + fi * gi, fr * gi - fi * gr)
-        put_rows(h, y)
-    pack(1)
-    own4 = scatter(ret_snd.at[1], ret_rcv.at[1], 3)
-    for c in range(CHANS):
-        tap_sums(0, c, plane(4, c) * mixed_rows[c])
-        pgrad = rows[pl.ds(c, count, stride=CHANS), :].astype(BF16).astype(F32)
-        tap_sums(1, c, pgrad * qkv[2, c])
-        tap_sums(2, c, pgrad * qkv[1, c])
+        put_rows(0, inverse(fr * gr + fi * gi, fr * gi - fi * gr))
+        put_rows(1, inverse(pr * gr + pi * gi, pr * gi - pi * gr) * scale)
+        pack(1 + h)
+        own4.append(scatter(ret_snd.at[1 + h], ret_rcv.at[1 + h], 3 + h))
+        for n, c in enumerate(pair):
+            tap_sums(0, c, plane(4, c) * mixed_rows[c])
+            pgrad = rows[pl.ds(n, count, stride=CHANS), :].astype(BF16).astype(F32)
+            tap_sums(1, c, pgrad * qkv[2, c])
+            tap_sums(2, c, pgrad * qkv[1, c])
     entries = jnp.sum(sums[...], 1)
     row = lax.dot_general(
         jnp.ones((8, TILE), F32), entries, (((1,), (1,)), ((), ())),
         precision=lax.Precision.HIGHEST, preferred_element_type=F32,
     )
     small[...] = row[0:1] * scale
-    for h in range(2):
-        pr, pi = spectrum(0, h)
-        gr, gi = spectrum(2, h)
-        put_rows(h, inverse(pr * gr + pi * gi, pr * gi - pi * gr) * scale)
-    pack(2)
-    own5 = pltpu.make_async_copy(ret_snd.at[2].at[me], fgrad_raw.at[me], own_sem.at[4])
-    own5.start()
     own6 = pltpu.make_async_copy(small, tall.at[me], own_sem.at[5])
     own6.start()
-
-    def last(peer):
-        remote(ret_snd.at[2].at[peer], fgrad_raw.at[me], 4, peer).start()
-        remote(small, tall.at[me], 5, peer).start()
-
-    each_peer(last)
-
-    strips = [pl.ds(q * TILE, TILE) for q in range(ext.shape[2] // TILE)]
+    each_peer(lambda peer: remote(small, tall.at[me], 5, peer).start())
+
+    strips = [pl.ds(q * TILE, TILE) for q in range(width // TILE)]
+
+    def edges(part, sem):
+        inner, beyond = cgrad.at[part, pl.ds(0, 8)], cgrad.at[part, pl.ds(TILE, 8)]
+        return remote(inner, beyond, sem, lax.rem(me + count - 1, count)), remote(inner, beyond, sem, me)
+
+    def send_edges(edge_out):
+        @pl.when(me > 0)
+        def _():
+            edge_out.start()
+
+    def get_edges(edge_in):
+        @pl.when(me < count - 1)
+        def _():
+            edge_in.wait_recv()
+
+    def correlate(streams, first, number):
+        for i in streams:
+            for lanes in strips:
+                total = None
+                for j in range(reach + 1):
+                    term = taps[i, pl.ds(j, 1), lanes] * cgrad[i, pl.ds(first + j, number), lanes]
+                    total = term if total is None else total + term
+                sgrad_ref[i, pl.ds(first, number), lanes] = total.astype(BF16)
+
+    @pl.when(me == count - 1)
+    def _():
+        cgrad[:, pl.ds(TILE, 8), :] = jnp.zeros((3, 8, width), F32)
+
+    edge_out0, edge_in0 = edges(pl.ds(0, 1), 7)
+    edge_out1, edge_in1 = edges(pl.ds(1, 2), 2 + 8)
     own3.wait()
     others(ret_snd.at[0], ret_rcv.at[0], 2).wait_recv()
     for q, lanes in enumerate(strips):
         mixed = turn_back(ret_rcv.at[0], q)
         gated_ref[:, lanes] = (local_qkv[0, :, lanes] * mixed).astype(BF16)
         cgrad[0, pl.ds(0, TILE), lanes] = ct[:, lanes].astype(F32) * mixed
-    own4.wait()
-    others(ret_snd.at[1], ret_rcv.at[1], 3).wait_recv()
+    send_edges(edge_out0)
+    correlate((0,), 0, TILE - 16)
+    for h in range(2):
+        own4[h].wait()
+        others(ret_snd.at[1 + h], ret_rcv.at[1 + h], 3 + h).wait_recv()
     for q, lanes in enumerate(strips):
-        pgrad = turn_back(ret_rcv.at[1], q)
+        pgrad = jnp.where(low, turn_back(ret_rcv.at[1], q), pltpu.roll(turn_back(ret_rcv.at[2], q), 2, 1))
         cgrad[1, pl.ds(0, TILE), lanes] = pgrad * local_qkv[2, :, lanes]
         cgrad[2, pl.ds(0, TILE), lanes] = pgrad * local_qkv[1, :, lanes]
-    edge = cgrad.at[:, pl.ds(0, 8)]
-    beyond = cgrad.at[:, pl.ds(TILE, 8)]
-    edge_out = remote(edge, beyond, 7, lax.rem(me + count - 1, count))
-    edge_in = remote(edge, beyond, 7, me)
-
-    @pl.when(me > 0)
-    def _():
-        edge_out.start()
-
-    def correlate(first, number):
-        for i in range(3):
-            for lanes in strips:
-                total = None
-                for j in range(reach + 1):
-                    term = taps[i, pl.ds(j, 1), lanes] * cgrad[i, pl.ds(first + j, number), lanes]
-                    total = term if total is None else total + term
-                sgrad_ref[i, pl.ds(first, number), lanes] = total.astype(BF16)
-
-    correlate(0, TILE - 16)
-
-    @pl.when(me < count - 1)
-    def _():
-        edge_in.wait_recv()
-
-    @pl.when(me == count - 1)
-    def _():
-        cgrad[:, pl.ds(TILE, 8), :] = jnp.zeros((3, 8, width), F32)
-
-    correlate(TILE - 16, 16)
-    own5.wait()
-    others(ret_snd.at[2], fgrad_raw, 4).wait_recv()
+    send_edges(edge_out1)
+    for q, lanes in enumerate(strips):
+        fgrad = jnp.where(low, pltpu.roll(turn_back(ret_rcv.at[1], q), TILE - 2, 1), turn_back(ret_rcv.at[2], q))
+        fgrad_ref[:, lanes] = fgrad.astype(BF16)
+    correlate((1, 2), 0, TILE - 16)
+    get_edges(edge_in0)
+    correlate((0,), TILE - 16, 16)
+    get_edges(edge_in1)
+    correlate((1, 2), TILE - 16, 16)
     own6.wait()
     others(tall, tall, 5).wait_recv()
     others(snd1, rcv1, 0).wait_send()
     for k, sem in enumerate(LATER):
         others(snd2.at[k], rcv2.at[k], sem).wait_send()
-    for k in range(2):
+    for k in range(3):
         others(ret_snd.at[k], ret_rcv.at[k], 2 + k).wait_send()
-    others(ret_snd.at[2], fgrad_raw, 4).wait_send()
     others(tall, tall, 5).wait_send()
 
     @pl.when(me < count - 1)
@@ -344,11 +365,12 @@
 
     @pl.when(me > 0)
     def _():
-        edge_out.wait_send()
+        edge_out0.wait_send()
+        edge_out1.wait_send()
 
 
 def result_kernel(
-    gated, sgrad, fgrad_raw, tall, gated_hbm, sgrad_hbm, fgrad_hbm, tgrad_hbm, fgrad, tgrad, spread, sem
+    gated, sgrad, fgrad, tall, gated_hbm, sgrad_hbm, fgrad_hbm, tgrad_hbm, tgrad, spread, sem
 ):
     count = tall.shape[0]
     terms = tgrad.shape[1]
@@ -358,11 +380,8 @@
             ((gated, gated_hbm), (sgrad, sgrad_hbm), (fgrad, fgrad_hbm), (tgrad, tgrad_hbm))
         )
     ]
-    stores[0].start()
-    stores[1].start()
-    for q in range(fgrad.shape[1] // TILE):
-        fgrad[:, q * TILE : (q + 1) * TILE] = turn_back(fgrad_raw, q).astype(BF16)
-    stores[2].start()
+    for store in stores[:3]:
+        store.start()
     entries = tall[...].reshape(count, TILE)
     for c in range(CHANS):
         moved = pltpu.roll(entries, TILE - c * ENTRIES, 1) if c else entries
@@ -379,7 +398,7 @@
 def local(streams, taps, filters, cotangent):
     rows, width = filters.shape
     count = lax.axis_size("ctx")
-    assert rows == TILE and width == CHANS * count and count == TILE
+    assert rows == TILE and width == CHANS * count and count == TILE == Y_SIZE * Z_SIZE * X_SIZE
     tables = [jnp.asarray(t) for t in make_tables(count, rows)]
     reach = taps.shape[1] - 1
     hbm = pl.BlockSpec(memory_space=pltpu.HBM)
@@ -396,21 +415,21 @@
         VMEM((3, CHANS, count, TILE), F32),
         VMEM((3, 2, 2 * count, 2 * TILE), F32),
         VMEM((count * CHANS, TILE), F32), VMEM((CHANS, count, TILE), F32),
-        VMEM((3,) + line, BF16), VMEM((2,) + line, BF16),
+        VMEM((3,) + line, BF16), VMEM((3,) + line, BF16),
         VMEM((TILE, 8, TILE), F32), VMEM((1, TILE), F32),
         VMEM((3, 16, width), BF16),
         VMEM((3, 8 + TILE, width), F32),
         VMEM((3, TILE, width), F32),
         VMEM((3, TILE + 8, width), F32),
         pltpu.SemaphoreType.DMA((9,)), pltpu.SemaphoreType.DMA((10,)),
-        pltpu.SemaphoreType.DMA((10,)), pltpu.SemaphoreType.DMA((10,)),
+        pltpu.SemaphoreType.DMA((11,)), pltpu.SemaphoreType.DMA((11,)),
     ]
     parts = pl.pallas_call(
         block_kernel,
         out_shape=[
             jax.ShapeDtypeStruct(cotangent.shape, BF16),
             jax.ShapeDtypeStruct(streams.shape, BF16),
-            jax.ShapeDtypeStruct(line, BF16),
+            jax.ShapeDtypeStruct(filters.shape, BF16),
             jax.ShapeDtypeStruct((count, 1, TILE), F32),
         ],
         in_specs=[hbm] * 9,
@@ -431,7 +450,7 @@
         in_specs=[vmem] * 4,
         out_specs=[hbm] * 4,
         scratch_shapes=[
-            VMEM(filters.shape, BF16), VMEM(taps.shape, F32), VMEM((count * CHANS, TILE), F32),
+            VMEM(taps.shape, F32), VMEM((count * CHANS, TILE), F32),
             pltpu.SemaphoreType.DMA((4,)),
         ],
         compiler_params=pltpu.CompilerParams(vmem_limit_bytes=8 << 20),

time: 54.5 us -> 55.2 us (1.013)
  Pallas kernels: 53.7 us -> 54.4 us
    pallas_call x1, Pallas kernels: 52.8 us -> 53.5 us  [local(): pl.pallas_call(block_kernel, out_shape=[jax.ShapeDtypeStruct(cotangent.sh...]
where the time goes in v4:
time: 55.2 us; the launch traced here: 55.1 us
  Pallas kernels  54.4 us (99%)
  between operations  0.64 us (1%)
    pallas_call x1, Pallas kernels, local(): pl.pallas_call(block_kernel, out_shape=[jax.ShapeDtypeStruct(cotangent.sh...  53.5 us

profile of v4, /device:TPU:6, one launch (start us, length us, event | category | flops | bytes accessed | tf_op | source)
XLA Modules:
  0.0 55.1 jit_solution(13254133457127302436)
XLA Ops:
  0.6 53.5 %shard_map.120 = (bf16[128,512]{1,0:T(8,128)(2,1)S(1)}, bf16[3,128,512]{2,1,0:T(8,128)(2,1)S(1)}, bf16[128,512]{1,0:T(8,128)(2,1)S(1)}, f32[128,1,128]{2,1,0:T(1,128)S(1)}) custom-call(bf16[3,128,512]{2,1,0:T(8,128)(2,1)} %streams_hbm.1, bf16[128,512]{1,0:T(8,128)(2,1)} %filters_hbm.1, bf16[128,512]{1,0:T(8,128)(2,1)} %cot_hbm.1, f32[3,7,512]{2,1,0:T(8,128)} %taps_hbm.1, ...), custom_call_target="tpu_custom_call" | custom-call | tf_op jit(solution)/shard_map/pallas_call | solution.py:427
  54.2 0.9 %shard_map.121 = (bf16[128,512]{1,0:T(8,128)(2,1)}, bf16[3,128,512]{2,1,0:T(8,128)(2,1)}, bf16[128,512]{1,0:T(8,128)(2,1)}, f32[3,7,512]{2,1,0:T(8,128)}) custom-call(bf16[128,512]{1,0:T(8,128)(2,1)S(1)} %get-tuple-element.8.gated, bf16[3,128,512]{2,1,0:T(8,128)(2,1)S(1)} %get-tuple-element.9.sgrad, bf16[128,512]{1,0:T(8,128)(2,1)S(1)} %get-tuple-element.10.fgrad, ...), custom_call_target="tpu_custom_call" | custom-call | tf_op jit(solution)/shard_map/pallas_call | solution.py:442

commit v5 on v4

--- a/solution.py
+++ b/solution.py
@@ -14,9 +14,10 @@
 BF16 = jnp.bfloat16
 CHANS = 4
 TILE = 128
-ENTRIES = 24
+ENTRIES = 32
+AHEAD = 24
 Y_SIZE, Z_SIZE, X_SIZE = 8, 8, 2
-LATER = (1, 8, 9)
+LATER = (1, 8, 10)
 
 
 def halves(table):
@@ -55,10 +56,10 @@
 
 def block_kernel(
     streams_hbm, filters_hbm, cot_hbm, taps_hbm, e1_hbm, e2_hbm, e2t_hbm, back_hbm, tw_hbm,
-    gated_ref, sgrad_ref, fgrad_ref, tall,
+    gated_ref, sgrad_ref, fgrad_ref, tgrad_ref,
     st, fl, ct, taps, e1, e2, e2t, back, tw,
-    snd1, snd2, rcv1, rcv2, own_taps, grid, shifts, qkv, spec, rows, mixed_rows, ret_snd, ret_rcv,
-    sums, small, halo, ext, local_qkv, cgrad,
+    snd1, snd2, rcv1, rcv2, own_taps, grid, shifts, qkv, spec, rows, mixed_rows, pgrad_rows, ret_snd, ret_rcv,
+    sums, small, tall, spread, halo, halo_next, ext, local_qkv, cgrad,
     in_sem, own_sem, send_sem, recv_sem,
 ):
     count = rcv1.shape[0]
@@ -156,15 +157,23 @@
     halo_out = remote(st.at[:, pl.ds(TILE - 16, 16)], halo, 6, lax.rem(me + 1, count))
     halo_in = remote(st.at[:, pl.ds(TILE - 16, 16)], halo, 6, me)
 
+    next_out = remote(st.at[pl.ds(1, 2), pl.ds(0, 16)], halo_next, 4 + 5, lax.rem(me + count - 1, count))
+    next_in = remote(st.at[pl.ds(1, 2), pl.ds(0, 16)], halo_next, 4 + 5, me)
+
     @pl.when(me < count - 1)
     def _():
         halo_out.start()
+
+    @pl.when(me > 0)
+    def _():
+        next_out.start()
 
     own1 = scatter(snd1, rcv1, 0)
     own2 = [scatter(snd2.at[k], rcv2.at[k], sem) for k, sem in enumerate(LATER)]
 
     sums[...] = jnp.zeros_like(sums)
     grid[:, pl.ds(0, 8), :] = jnp.zeros((5, 8, TILE), F32)
+    pgrad_rows[:, pl.ds(count, 8), :] = jnp.zeros((CHANS, 8, TILE), F32)
     ext[:, pl.ds(8, TILE), :] = st[...].astype(F32)
 
     @pl.when(me > 0)
@@ -176,14 +185,24 @@
     def _():
         ext[:, pl.ds(0, 8), :] = jnp.zeros((3, 8, ext.shape[2]), F32)
 
+    @pl.when(me < count - 1)
+    def _():
+        next_in.wait_recv()
+        ext[pl.ds(1, 2), pl.ds(8 + TILE, 8), :] = halo_next[...].astype(F32)[:, :8, :]
+
+    @pl.when(me == count - 1)
+    def _():
+        ext[pl.ds(1, 2), pl.ds(8 + TILE, 8), :] = jnp.zeros((2, 8, width), F32)
+
     for i in range(3):
-        for q in range(ext.shape[2] // TILE):
+        number = TILE + 8 if i else TILE
+        for q in range(width // TILE):
             lanes = pl.ds(q * TILE, TILE)
             total = None
             for j in range(reach + 1):
-                term = taps[i, pl.ds(j, 1), lanes] * ext[i, pl.ds(8 - j, TILE), lanes]
+                term = taps[i, pl.ds(j, 1), lanes] * ext[i, pl.ds(8 - j, number), lanes]
                 total = term if total is None else total + term
-            local_qkv[i, :, lanes] = total
+            local_qkv[i, pl.ds(0, number), lanes] = total
 
     def slot(index, c):
         if index in (1, 2, 3):
@@ -276,40 +295,35 @@
         pr, pi = spectrum(0, h)
         fr, fi = spectrum(1, h)
         gr, gi = spectrum(2, h)
-        put_rows(0, inverse(fr * gr + fi * gi, fr * gi - fi * gr))
+        pgrad = inverse(fr * gr + fi * gi, fr * gi - fi * gr)
+        put_rows(0, pgrad)
         put_rows(1, inverse(pr * gr + pi * gi, pr * gi - pi * gr) * scale)
         pack(1 + h)
         own4.append(scatter(ret_snd.at[1 + h], ret_rcv.at[1 + h], 3 + h))
         for n, c in enumerate(pair):
-            tap_sums(0, c, plane(4, c) * mixed_rows[c])
-            pgrad = rows[pl.ds(n, count, stride=CHANS), :].astype(BF16).astype(F32)
-            tap_sums(1, c, pgrad * qkv[2, c])
-            tap_sums(2, c, pgrad * qkv[1, c])
+            pgrad_rows[c, pl.ds(0, count), :] = pgrad[:, n * TILE : (n + 1) * TILE].astype(BF16).astype(F32)
+    ahead = None
+    for c in range(CHANS):
+        tap_sums(0, c, plane(4, c) * mixed_rows[c])
+        tap_sums(1, c, pgrad_rows[c, pl.ds(0, count), :] * qkv[2, c])
+        tap_sums(2, c, pgrad_rows[c, pl.ds(0, count), :] * qkv[1, c])
+        place = c * ENTRIES + AHEAD
+        moved = pltpu.roll(pgrad_rows[c, pl.ds(1, count), :], place, 1)
+        moved = jnp.where((lane >= place) & (lane < place + reach), moved, 0.0)
+        ahead = moved if ahead is None else ahead + moved
     entries = jnp.sum(sums[...], 1)
     row = lax.dot_general(
         jnp.ones((8, TILE), F32), entries, (((1,), (1,)), ((), ())),
         precision=lax.Precision.HIGHEST, preferred_element_type=F32,
     )
-    small[...] = row[0:1] * scale
-    own6 = pltpu.make_async_copy(small, tall.at[me], own_sem.at[5])
-    own6.start()
-    each_peer(lambda peer: remote(small, tall.at[me], 5, peer).start())
+    small[...] = (row[0:1] * scale + ahead).reshape(count, 1, TILE)
+    own6 = scatter(small, tall, 5)
 
     strips = [pl.ds(q * TILE, TILE) for q in range(width // TILE)]
 
-    def edges(part, sem):
-        inner, beyond = cgrad.at[part, pl.ds(0, 8)], cgrad.at[part, pl.ds(TILE, 8)]
-        return remote(inner, beyond, sem, lax.rem(me + count - 1, count)), remote(inner, beyond, sem, me)
-
-    def send_edges(edge_out):
-        @pl.when(me > 0)
-        def _():
-            edge_out.start()
-
-    def get_edges(edge_in):
-        @pl.when(me < count - 1)
-        def _():
-            edge_in.wait_recv()
+    edge, beyond = cgrad.at[0, pl.ds(0, 8)], cgrad.at[0, pl.ds(TILE, 8)]
+    edge_out = remote(edge, beyond, 7, lax.rem(me + count - 1, count))
+    edge_in = remote(edge, beyond, 7, me)
 
     def correlate(streams, first, number):
         for i in streams:
@@ -322,42 +336,58 @@
 
     @pl.when(me == count - 1)
     def _():
-        cgrad[:, pl.ds(TILE, 8), :] = jnp.zeros((3, 8, width), F32)
-
-    edge_out0, edge_in0 = edges(pl.ds(0, 1), 7)
-    edge_out1, edge_in1 = edges(pl.ds(1, 2), 2 + 8)
+        cgrad[0, pl.ds(TILE, 8), :] = jnp.zeros((8, width), F32)
+
     own3.wait()
     others(ret_snd.at[0], ret_rcv.at[0], 2).wait_recv()
     for q, lanes in enumerate(strips):
         mixed = turn_back(ret_rcv.at[0], q)
-        gated_ref[:, lanes] = (local_qkv[0, :, lanes] * mixed).astype(BF16)
+        gated_ref[:, lanes] = (local_qkv[0, pl.ds(0, TILE), lanes] * mixed).astype(BF16)
         cgrad[0, pl.ds(0, TILE), lanes] = ct[:, lanes].astype(F32) * mixed
-    send_edges(edge_out0)
+
+    @pl.when(me > 0)
+    def _():
+        edge_out.start()
+
     correlate((0,), 0, TILE - 16)
     for h in range(2):
         own4[h].wait()
         others(ret_snd.at[1 + h], ret_rcv.at[1 + h], 3 + h).wait_recv()
     for q, lanes in enumerate(strips):
         pgrad = jnp.where(low, turn_back(ret_rcv.at[1], q), pltpu.roll(turn_back(ret_rcv.at[2], q), 2, 1))
-        cgrad[1, pl.ds(0, TILE), lanes] = pgrad * local_qkv[2, :, lanes]
-        cgrad[2, pl.ds(0, TILE), lanes] = pgrad * local_qkv[1, :, lanes]
-    send_edges(edge_out1)
+        cgrad[1, pl.ds(0, TILE), lanes] = pgrad * local_qkv[2, pl.ds(0, TILE), lanes]
+        cgrad[2, pl.ds(0, TILE), lanes] = pgrad * local_qkv[1, pl.ds(0, TILE), lanes]
     for q, lanes in enumerate(strips):
         fgrad = jnp.where(low, pltpu.roll(turn_back(ret_rcv.at[1], q), TILE - 2, 1), turn_back(ret_rcv.at[2], q))
         fgrad_ref[:, lanes] = fgrad.astype(BF16)
     correlate((1, 2), 0, TILE - 16)
-    get_edges(edge_in0)
+
+    @pl.when(me < count - 1)
+    def _():
+        edge_in.wait_recv()
+
     correlate((0,), TILE - 16, 16)
-    get_edges(edge_in1)
+    own6.wait()
+    others(small, tall, 5).wait_recv()
+    shared = tall[...].reshape(count, TILE)
+    for c in range(CHANS):
+        moved = pltpu.roll(shared, TILE - c * ENTRIES, 1) if c else shared
+        spread[pl.ds(c, count, stride=CHANS), :] = moved
+    terms = reach + 1
+    for q, lanes in enumerate(strips):
+        by_entry = spread[pl.ds(q * TILE, TILE), :].T
+        for i in range(3):
+            tgrad_ref[i, :, lanes] = by_entry[i * terms : (i + 1) * terms]
+        following = by_entry[AHEAD : AHEAD + 8]
+        cgrad[1, pl.ds(TILE, 8), lanes] = following * local_qkv[2, pl.ds(TILE, 8), lanes]
+        cgrad[2, pl.ds(TILE, 8), lanes] = following * local_qkv[1, pl.ds(TILE, 8), lanes]
     correlate((1, 2), TILE - 16, 16)
-    own6.wait()
-    others(tall, tall, 5).wait_recv()
     others(snd1, rcv1, 0).wait_send()
     for k, sem in enumerate(LATER):
         others(snd2.at[k], rcv2.at[k], sem).wait_send()
     for k in range(3):
         others(ret_snd.at[k], ret_rcv.at[k], 2 + k).wait_send()
-    others(tall, tall, 5).wait_send()
+    others(small, tall, 5).wait_send()
 
     @pl.when(me < count - 1)
     def _():
@@ -365,32 +395,19 @@
 
     @pl.when(me > 0)
     def _():
-        edge_out0.wait_send()
-        edge_out1.wait_send()
-
-
-def result_kernel(
-    gated, sgrad, fgrad, tall, gated_hbm, sgrad_hbm, fgrad_hbm, tgrad_hbm, tgrad, spread, sem
-):
-    count = tall.shape[0]
-    terms = tgrad.shape[1]
+        next_out.wait_send()
+        edge_out.wait_send()
+
+
+def result_kernel(*refs):
+    number = len(refs) // 2
+    sem = refs[-1]
     stores = [
         pltpu.make_async_copy(source, target, sem.at[i])
-        for i, (source, target) in enumerate(
-            ((gated, gated_hbm), (sgrad, sgrad_hbm), (fgrad, fgrad_hbm), (tgrad, tgrad_hbm))
-        )
+        for i, (source, target) in enumerate(zip(refs[:number], refs[number : 2 * number]))
     ]
-    for store in stores[:3]:
+    for store in stores:
         store.start()
-    entries = tall[...].reshape(count, TILE)
-    for c in range(CHANS):
-        moved = pltpu.roll(entries, TILE - c * ENTRIES, 1) if c else entries
-        spread[pl.ds(c, count, stride=CHANS), :] = moved
-    for q in range(fgrad.shape[1] // TILE):
-        by_entry = spread[q * TILE : (q + 1) * TILE, :].T
-        for i in range(tgrad.shape[0]):
-            tgrad[i, :, q * TILE : (q + 1) * TILE] = by_entry[i * terms : (i + 1) * terms]
-    stores[3].start()
     for store in stores:
         store.wait()
 
@@ -414,14 +431,15 @@
         VMEM((3, CHANS, reach + 1, count, TILE), F32),
         VMEM((3, CHANS, count, TILE), F32),
         VMEM((3, 2, 2 * count, 2 * TILE), F32),
-        VMEM((count * CHANS, TILE), F32), VMEM((CHANS, count, TILE), F32),
+        VMEM((count * CHANS, TILE), F32), VMEM((CHANS, count, TILE), F32), VMEM((CHANS, count + 8, TILE), F32),
         VMEM((3,) + line, BF16), VMEM((3,) + line, BF16),
-        VMEM((TILE, 8, TILE), F32), VMEM((1, TILE), F32),
-        VMEM((3, 16, width), BF16),
-        VMEM((3, 8 + TILE, width), F32),
-        VMEM((3, TILE, width), F32),
+        VMEM((TILE, 8, TILE), F32), VMEM((count, 1, TILE), F32), VMEM((count, 1, TILE), F32),
+        VMEM((count * CHANS, TILE), F32),
+        VMEM((3, 16, width), BF16), VMEM((2, 16, width), BF16),
+        VMEM((3, 8 + TILE + 8, width), F32),
         VMEM((3, TILE + 8, width), F32),
-        pltpu.SemaphoreType.DMA((9,)), pltpu.SemaphoreType.DMA((10,)),
+        VMEM((3, TILE + 8, width), F32),
+        pltpu.SemaphoreType.DMA((9,)), pltpu.SemaphoreType.DMA((11,)),
         pltpu.SemaphoreType.DMA((11,)), pltpu.SemaphoreType.DMA((11,)),
     ]
     parts = pl.pallas_call(
@@ -430,7 +448,7 @@
             jax.ShapeDtypeStruct(cotangent.shape, BF16),
             jax.ShapeDtypeStruct(streams.shape, BF16),
             jax.ShapeDtypeStruct(filters.shape, BF16),
-            jax.ShapeDtypeStruct((count, 1, TILE), F32),
+            jax.ShapeDtypeStruct(taps.shape, F32),
         ],
         in_specs=[hbm] * 9,
         out_specs=[vmem] * 4,
@@ -449,10 +467,7 @@
         ],
         in_specs=[vmem] * 4,
         out_specs=[hbm] * 4,
-        scratch_shapes=[
-            VMEM(taps.shape, F32), VMEM((count * CHANS, TILE), F32),
-            pltpu.SemaphoreType.DMA((4,)),
-        ],
+        scratch_shapes=[pltpu.SemaphoreType.DMA((4,))],
         compiler_params=pltpu.CompilerParams(vmem_limit_bytes=8 << 20),
     )(*parts)
 

time: 55.2 us -> 53.6 us (0.971)
  Pallas kernels: 54.4 us -> 52.8 us
    pallas_call x1, Pallas kernels: 53.5 us -> 51.9 us  [local(): pl.pallas_call(block_kernel, out_shape=[jax.ShapeDtypeStruct(cotangent.sh...]
where the time goes in v5:
time: 53.6 us; the launch traced here: 53.4 us
  Pallas kernels  52.8 us (99%)
  between operations  0.64 us (1%)
    pallas_call x1, Pallas kernels, local(): pl.pallas_call(block_kernel, out_shape=[jax.ShapeDtypeStruct(cotangent.sh...  51.9 us

profile of v5, /device:TPU:6, one launch (start us, length us, event | category | flops | bytes accessed | tf_op | source)
XLA Modules:
  0.0 53.4 jit_solution(13443672691889826426)
XLA Ops:
  0.6 51.9 %shard_map.120 = (bf16[128,512]{1,0:T(8,128)(2,1)S(1)}, bf16[3,128,512]{2,1,0:T(8,128)(2,1)S(1)}, bf16[128,512]{1,0:T(8,128)(2,1)S(1)}, f32[3,7,512]{2,1,0:T(8,128)S(1)}) custom-call(bf16[3,128,512]{2,1,0:T(8,128)(2,1)} %streams_hbm.1, bf16[128,512]{1,0:T(8,128)(2,1)} %filters_hbm.1, bf16[128,512]{1,0:T(8,128)(2,1)} %cot_hbm.1, f32[3,7,512]{2,1,0:T(8,128)} %taps_hbm.1, ...), custom_call_target="tpu_custom_call" | custom-call | tf_op jit(solution)/shard_map/pallas_call | solution.py:445
  52.6 0.9 %shard_map.121 = (bf16[128,512]{1,0:T(8,128)(2,1)}, bf16[3,128,512]{2,1,0:T(8,128)(2,1)}, bf16[128,512]{1,0:T(8,128)(2,1)}, f32[3,7,512]{2,1,0:T(8,128)}) custom-call(bf16[128,512]{1,0:T(8,128)(2,1)S(1)} %get-tuple-element.8.refs_0_, bf16[3,128,512]{2,1,0:T(8,128)(2,1)S(1)} %get-tuple-element.9.refs_1_, bf16[128,512]{1,0:T(8,128)(2,1)S(1)} %get-tuple-element.10.refs_2_, ...), custom_call_target="tpu_custom_call" | custom-call | tf_op jit(solution)/shard_map/pallas_call | solution.py:460

commit v6 on v5

--- a/solution.py
+++ b/solution.py
@@ -37,7 +37,8 @@
     e1 = np.concatenate(halves(e1), 1)
     e2, e2t, back = (np.stack(halves(x)) for x in (e2, e2.T, back))
     twist = np.stack([np.tile(x, (1, 2)) for x in (twist.real, twist.imag)]).astype(np.float32)
-    return e1, e2, e2t, back, twist
+    stacked = np.concatenate([x.reshape(-1, 2 * b_size) for x in (e1, e2, e2t, back)], 0)
+    return stacked, twist
 
 
 def dot(a, b):
@@ -55,12 +56,12 @@
 
 
 def block_kernel(
-    streams_hbm, filters_hbm, cot_hbm, taps_hbm, e1_hbm, e2_hbm, e2t_hbm, back_hbm, tw_hbm,
+    streams_hbm, filters_hbm, cot_hbm, taps_hbm, dft_hbm, tw_hbm,
     gated_ref, sgrad_ref, fgrad_ref, tgrad_ref,
-    st, fl, ct, taps, e1, e2, e2t, back, tw,
+    st, fl, ct, taps, dft, tw,
     snd1, snd2, rcv1, rcv2, own_taps, grid, shifts, qkv, spec, rows, mixed_rows, pgrad_rows, ret_snd, ret_rcv,
     sums, small, tall, spread, halo, halo_next, ext, local_qkv, cgrad,
-    in_sem, own_sem, send_sem, recv_sem,
+    in_sem, send_sem, recv_sem,
 ):
     count = rcv1.shape[0]
     width = ext.shape[2]
@@ -100,8 +101,8 @@
         pltpu.make_async_copy(source, target, in_sem.at[i])
         for i, (source, target) in enumerate(
             (
-                (streams_hbm, st), (filters_hbm, fl), (cot_hbm, ct), (taps_hbm, taps), (e1_hbm, e1),
-                (e2_hbm, e2), (e2t_hbm, e2t), (back_hbm, back), (tw_hbm, tw),
+                (streams_hbm, st), (filters_hbm, fl), (cot_hbm, ct), (taps_hbm, taps), (dft_hbm, dft),
+                (tw_hbm, tw),
             )
         )
     ]
@@ -145,10 +146,8 @@
             own_taps[c, i, pl.ds(0, reach + 1), :] = jnp.broadcast_to(tap, (reach + 1, TILE))
 
     def scatter(source, target, sem):
-        own = pltpu.make_async_copy(source.at[me], target.at[me], own_sem.at[sem])
-        own.start()
         each_peer(lambda peer: remote(source.at[peer], target.at[me], sem, peer).start())
-        return own
+        target[me] = source[me]
 
     def others(source, target, sem):
         return remote(source.at[pl.ds(0, count - 1)], target.at[pl.ds(0, count - 1)], sem, me)
@@ -168,8 +167,9 @@
     def _():
         next_out.start()
 
-    own1 = scatter(snd1, rcv1, 0)
-    own2 = [scatter(snd2.at[k], rcv2.at[k], sem) for k, sem in enumerate(LATER)]
+    scatter(snd1, rcv1, 0)
+    for k, sem in enumerate(LATER):
+        scatter(snd2.at[k], rcv2.at[k], sem)
 
     sums[...] = jnp.zeros_like(sums)
     grid[:, pl.ds(0, 8), :] = jnp.zeros((5, 8, TILE), F32)
@@ -228,6 +228,12 @@
         qkv[index, c] = total
         return total
 
+    size = 2 * TILE
+    e1 = dft.at[pl.ds(0, size)]
+    e2 = [dft.at[pl.ds((1 + k) * size, size)] for k in range(2)]
+    e2t = [dft.at[pl.ds((3 + k) * size, size)] for k in range(2)]
+    back = [dft.at[pl.ds(5 * size + k * TILE, TILE)] for k in range(2)]
+
     def forward(planes, index, h):
         x = jnp.concatenate(planes, 1)
         y = dot(e1[...], jnp.concatenate([x, x], 0))
@@ -238,19 +244,19 @@
             [jnp.concatenate([v[:, n * TILE : (n + 1) * TILE] for v in (tre, tim)], 1) for n in range(2)], 0
         )
         high, low = split(turned)
-        spec[index, h] = dot(high, e2[0]) + dot(low, e2[0]) + dot(high, e2[1])
+        spec[index, h] = dot(high, e2[0][...]) + dot(low, e2[0][...]) + dot(high, e2[1][...])
 
     def spectrum(index, h):
         return spec[index, h, :, pl.ds(0, TILE)], spec[index, h, :, pl.ds(TILE, TILE)]
 
     def inverse(re, im):
         high, low = split(jnp.concatenate([re, im], 1))
-        u = dot(high, e2t[0]) + dot(low, e2t[0]) + dot(high, e2t[1])
+        u = dot(high, e2t[0][...]) + dot(low, e2t[0][...]) + dot(high, e2t[1][...])
         ur = jnp.concatenate([u[:count, :TILE], u[count:, :TILE]], 1)
         ui = jnp.concatenate([u[:count, TILE:], u[count:, TILE:]], 1)
         twr, twi = tw[0], tw[1]
         high, low = split(jnp.concatenate([ur * twr + ui * twi, ui * twr - ur * twi], 0))
-        return dot(back[0], high) + dot(back[1], high) + dot(back[0], low)
+        return dot(back[0][...], high) + dot(back[1][...], high) + dot(back[0][...], low)
 
     def put_rows(h, values):
         for n in range(2):
@@ -265,14 +271,12 @@
             part = jnp.sum((grad * moved).reshape(count // 8, 8, TILE), 0)
             sums[c * ENTRIES + index * (reach + 1) + j] = part
 
-    own1.wait()
     others(snd1, rcv1, 0).wait_recv()
     unpack(rcv1.at[:, 0], 1)
     unpack(rcv1.at[:, 1], 2)
     for h in range(2):
         products = [(convolve(1, c) * convolve(2, c)).astype(BF16) for c in (2 * h, 2 * h + 1)]
         forward(products, 0, h)
-    own2[0].wait()
     others(snd2.at[0], rcv2.at[0], LATER[0]).wait_recv()
     unpack(rcv2.at[0], 3)
     for h in range(2):
@@ -281,14 +285,12 @@
         fr, fi = spectrum(1, h)
         put_rows(h, inverse(pr * fr - pi * fi, pr * fi + pi * fr))
     pack(0)
-    own3 = scatter(ret_snd.at[0], ret_rcv.at[0], 2)
+    scatter(ret_snd.at[0], ret_rcv.at[0], 2)
 
     for c in range(CHANS):
         mixed_rows[c] = rows[pl.ds(c, count, stride=CHANS), :].astype(BF16).astype(F32)
-    own4 = []
     for h in range(2):
         pair = (2 * h, 2 * h + 1)
-        own2[1 + h].wait()
         others(snd2.at[1 + h], rcv2.at[1 + h], LATER[1 + h]).wait_recv()
         unpack(rcv2.at[1 + h], (0, 4)[h])
         forward([(plane(4, c) * convolve(0, c)).astype(BF16) for c in pair], 2, h)
@@ -299,7 +301,7 @@
         put_rows(0, pgrad)
         put_rows(1, inverse(pr * gr + pi * gi, pr * gi - pi * gr) * scale)
         pack(1 + h)
-        own4.append(scatter(ret_snd.at[1 + h], ret_rcv.at[1 + h], 3 + h))
+        scatter(ret_snd.at[1 + h], ret_rcv.at[1 + h], 3 + h)
         for n, c in enumerate(pair):
             pgrad_rows[c, pl.ds(0, count), :] = pgrad[:, n * TILE : (n + 1) * TILE].astype(BF16).astype(F32)
     ahead = None
@@ -317,7 +319,7 @@
         precision=lax.Precision.HIGHEST, preferred_element_type=F32,
     )
     small[...] = (row[0:1] * scale + ahead).reshape(count, 1, TILE)
-    own6 = scatter(small, tall, 5)
+    scatter(small, tall, 5)
 
     strips = [pl.ds(q * TILE, TILE) for q in range(width // TILE)]
 
@@ -338,7 +340,6 @@
     def _():
         cgrad[0, pl.ds(TILE, 8), :] = jnp.zeros((8, width), F32)
 
-    own3.wait()
     others(ret_snd.at[0], ret_rcv.at[0], 2).wait_recv()
     for q, lanes in enumerate(strips):
         mixed = turn_back(ret_rcv.at[0], q)
@@ -351,7 +352,6 @@
 
     correlate((0,), 0, TILE - 16)
     for h in range(2):
-        own4[h].wait()
         others(ret_snd.at[1 + h], ret_rcv.at[1 + h], 3 + h).wait_recv()
     for q, lanes in enumerate(strips):
         pgrad = jnp.where(low, turn_back(ret_rcv.at[1], q), pltpu.roll(turn_back(ret_rcv.at[2], q), 2, 1))
@@ -367,7 +367,6 @@
         edge_in.wait_recv()
 
     correlate((0,), TILE - 16, 16)
-    own6.wait()
     others(small, tall, 5).wait_recv()
     shared = tall[...].reshape(count, TILE)
     for c in range(CHANS):
@@ -439,8 +438,7 @@
         VMEM((3, 8 + TILE + 8, width), F32),
         VMEM((3, TILE + 8, width), F32),
         VMEM((3, TILE + 8, width), F32),
-        pltpu.SemaphoreType.DMA((9,)), pltpu.SemaphoreType.DMA((11,)),
-        pltpu.SemaphoreType.DMA((11,)), pltpu.SemaphoreType.DMA((11,)),
+        pltpu.SemaphoreType.DMA((6,)), pltpu.SemaphoreType.DMA((11,)), pltpu.SemaphoreType.DMA((11,)),
     ]
     parts = pl.pallas_call(
         block_kernel,
@@ -450,7 +448,7 @@
             jax.ShapeDtypeStruct(filters.shape, BF16),
             jax.ShapeDtypeStruct(taps.shape, F32),
         ],
-        in_specs=[hbm] * 9,
+        in_specs=[hbm] * 6,
         out_specs=[vmem] * 4,
         scratch_shapes=scratch,
         compiler_params=pltpu.CompilerParams(

time: 53.6 us -> 53.6 us (level)
  no operation moved by 1% of the time
where the time goes in v6:
time: 53.6 us; the launch traced here: 53.5 us
  Pallas kernels  52.8 us (99%)
  between operations  0.64 us (1%)
    pallas_call x1, Pallas kernels, local(): pl.pallas_call(block_kernel, out_shape=[jax.ShapeDtypeStruct(cotangent.sh...  52 us

profile of v6, /device:TPU:6, one launch (start us, length us, event | category | flops | bytes accessed | tf_op | source)
XLA Modules:
  0.0 53.5 jit_solution(17688979232201149065)
XLA Ops:
  0.6 52.0 %shard_map.93 = (bf16[128,512]{1,0:T(8,128)(2,1)S(1)}, bf16[3,128,512]{2,1,0:T(8,128)(2,1)S(1)}, bf16[128,512]{1,0:T(8,128)(2,1)S(1)}, f32[3,7,512]{2,1,0:T(8,128)S(1)}) custom-call(bf16[3,128,512]{2,1,0:T(8,128)(2,1)} %streams_hbm.1, bf16[128,512]{1,0:T(8,128)(2,1)} %filters_hbm.1, bf16[128,512]{1,0:T(8,128)(2,1)} %cot_hbm.1, f32[3,7,512]{2,1,0:T(8,128)} %taps_hbm.1, ...), custom_call_target="tpu_custom_call" | custom-call | tf_op jit(solution)/shard_map/pallas_call | solution.py:443
  52.6 0.9 %shard_map.94 = (bf16[128,512]{1,0:T(8,128)(2,1)}, bf16[3,128,512]{2,1,0:T(8,128)(2,1)}, bf16[128,512]{1,0:T(8,128)(2,1)}, f32[3,7,512]{2,1,0:T(8,128)}) custom-call(bf16[128,512]{1,0:T(8,128)(2,1)S(1)} %get-tuple-element.8.refs_0_, bf16[3,128,512]{2,1,0:T(8,128)(2,1)S(1)} %get-tuple-element.9.refs_1_, bf16[128,512]{1,0:T(8,128)(2,1)S(1)} %get-tuple-element.10.refs_2_, ...), custom_call_target="tpu_custom_call" | custom-call | tf_op jit(solution)/shard_map/pallas_call | solution.py:458

commit v7 on v6

--- a/solution.py
+++ b/solution.py
@@ -153,11 +153,11 @@
         return remote(source.at[pl.ds(0, count - 1)], target.at[pl.ds(0, count - 1)], sem, me)
 
     pl.semaphore_wait(barrier, count - 1)
-    halo_out = remote(st.at[:, pl.ds(TILE - 16, 16)], halo, 6, lax.rem(me + 1, count))
-    halo_in = remote(st.at[:, pl.ds(TILE - 16, 16)], halo, 6, me)
-
-    next_out = remote(st.at[pl.ds(1, 2), pl.ds(0, 16)], halo_next, 4 + 5, lax.rem(me + count - 1, count))
-    next_in = remote(st.at[pl.ds(1, 2), pl.ds(0, 16)], halo_next, 4 + 5, me)
+    halo_out = remote(st.at[:, pl.ds(TILE - 8, 8)], halo, 6, lax.rem(me + 1, count))
+    halo_in = remote(st.at[:, pl.ds(TILE - 8, 8)], halo, 6, me)
+
+    next_out = remote(st.at[pl.ds(1, 2), pl.ds(0, 8)], halo_next, 4 + 5, lax.rem(me + count - 1, count))
+    next_in = remote(st.at[pl.ds(1, 2), pl.ds(0, 8)], halo_next, 4 + 5, me)
 
     @pl.when(me < count - 1)
     def _():
@@ -179,7 +179,7 @@
     @pl.when(me > 0)
     def _():
         halo_in.wait_recv()
-        ext[:, pl.ds(0, 8), :] = halo[...].astype(F32)[:, 8:, :]
+        ext[:, pl.ds(0, 8), :] = halo[...].astype(F32)
 
     @pl.when(me == 0)
     def _():
@@ -188,7 +188,7 @@
     @pl.when(me < count - 1)
     def _():
         next_in.wait_recv()
-        ext[pl.ds(1, 2), pl.ds(8 + TILE, 8), :] = halo_next[...].astype(F32)[:, :8, :]
+        ext[pl.ds(1, 2), pl.ds(8 + TILE, 8), :] = halo_next[...].astype(F32)
 
     @pl.when(me == count - 1)
     def _():
@@ -434,7 +434,7 @@
         VMEM((3,) + line, BF16), VMEM((3,) + line, BF16),
         VMEM((TILE, 8, TILE), F32), VMEM((count, 1, TILE), F32), VMEM((count, 1, TILE), F32),
         VMEM((count * CHANS, TILE), F32),
-        VMEM((3, 16, width), BF16), VMEM((2, 16, width), BF16),
+        VMEM((3, 8, width), BF16), VMEM((2, 8, width), BF16),
         VMEM((3, 8 + TILE + 8, width), F32),
         VMEM((3, TILE + 8, width), F32),
         VMEM((3, TILE + 8, width), F32),

time: 53.6 us -> 52 us (0.970)
  Pallas kernels: 52.8 us -> 51.3 us
    pallas_call x1, Pallas kernels: 52 us -> 50.4 us  [local(): pl.pallas_call(block_kernel, out_shape=[jax.ShapeDtypeStruct(cotangent.sh...]
where the time goes in v7:
time: 52 us; the launch traced here: 51.9 us
  Pallas kernels  51.3 us (99%)
  between operations  0.64 us (1%)
    pallas_call x1, Pallas kernels, local(): pl.pallas_call(block_kernel, out_shape=[jax.ShapeDtypeStruct(cotangent.sh...  50.4 us

profile of v7, /device:TPU:6, one launch (start us, length us, event | category | flops | bytes accessed | tf_op | source)
XLA Modules:
  0.0 51.9 jit_solution(3303621704528685454)
XLA Ops:
  0.6 50.4 %shard_map.93 = (bf16[128,512]{1,0:T(8,128)(2,1)S(1)}, bf16[3,128,512]{2,1,0:T(8,128)(2,1)S(1)}, bf16[128,512]{1,0:T(8,128)(2,1)S(1)}, f32[3,7,512]{2,1,0:T(8,128)S(1)}) custom-call(bf16[3,128,512]{2,1,0:T(8,128)(2,1)} %streams_hbm.1, bf16[128,512]{1,0:T(8,128)(2,1)} %filters_hbm.1, bf16[128,512]{1,0:T(8,128)(2,1)} %cot_hbm.1, f32[3,7,512]{2,1,0:T(8,128)} %taps_hbm.1, ...), custom_call_target="tpu_custom_call" | custom-call | tf_op jit(solution)/shard_map/pallas_call | solution.py:443
  51.0 0.9 %shard_map.94 = (bf16[128,512]{1,0:T(8,128)(2,1)}, bf16[3,128,512]{2,1,0:T(8,128)(2,1)}, bf16[128,512]{1,0:T(8,128)(2,1)}, f32[3,7,512]{2,1,0:T(8,128)}) custom-call(bf16[128,512]{1,0:T(8,128)(2,1)S(1)} %get-tuple-element.8.refs_0_, bf16[3,128,512]{2,1,0:T(8,128)(2,1)S(1)} %get-tuple-element.9.refs_1_, bf16[128,512]{1,0:T(8,128)(2,1)S(1)} %get-tuple-element.10.refs_2_, ...), custom_call_target="tpu_custom_call" | custom-call | tf_op jit(solution)/shard_map/pallas_call | solution.py:458

commit v8 on v7

--- a/solution.py
+++ b/solution.py
@@ -159,50 +159,21 @@
     next_out = remote(st.at[pl.ds(1, 2), pl.ds(0, 8)], halo_next, 4 + 5, lax.rem(me + count - 1, count))
     next_in = remote(st.at[pl.ds(1, 2), pl.ds(0, 8)], halo_next, 4 + 5, me)
 
-    @pl.when(me < count - 1)
-    def _():
-        halo_out.start()
-
-    @pl.when(me > 0)
-    def _():
-        next_out.start()
-
     scatter(snd1, rcv1, 0)
     for k, sem in enumerate(LATER):
         scatter(snd2.at[k], rcv2.at[k], sem)
 
+    @pl.when(me < count - 1)
+    def _():
+        halo_out.start()
+
+    @pl.when(me > 0)
+    def _():
+        next_out.start()
+
     sums[...] = jnp.zeros_like(sums)
     grid[:, pl.ds(0, 8), :] = jnp.zeros((5, 8, TILE), F32)
     pgrad_rows[:, pl.ds(count, 8), :] = jnp.zeros((CHANS, 8, TILE), F32)
-    ext[:, pl.ds(8, TILE), :] = st[...].astype(F32)
-
-    @pl.when(me > 0)
-    def _():
-        halo_in.wait_recv()
-        ext[:, pl.ds(0, 8), :] = halo[...].astype(F32)
-
-    @pl.when(me == 0)
-    def _():
-        ext[:, pl.ds(0, 8), :] = jnp.zeros((3, 8, ext.shape[2]), F32)
-
-    @pl.when(me < count - 1)
-    def _():
-        next_in.wait_recv()
-        ext[pl.ds(1, 2), pl.ds(8 + TILE, 8), :] = halo_next[...].astype(F32)
-
-    @pl.when(me == count - 1)
-    def _():
-        ext[pl.ds(1, 2), pl.ds(8 + TILE, 8), :] = jnp.zeros((2, 8, width), F32)
-
-    for i in range(3):
-        number = TILE + 8 if i else TILE
-        for q in range(width // TILE):
-            lanes = pl.ds(q * TILE, TILE)
-            total = None
-            for j in range(reach + 1):
-                term = taps[i, pl.ds(j, 1), lanes] * ext[i, pl.ds(8 - j, number), lanes]
-                total = term if total is None else total + term
-            local_qkv[i, pl.ds(0, number), lanes] = total
 
     def slot(index, c):
         if index in (1, 2, 3):
@@ -320,6 +291,36 @@
     )
     small[...] = (row[0:1] * scale + ahead).reshape(count, 1, TILE)
     scatter(small, tall, 5)
+
+    ext[:, pl.ds(8, TILE), :] = st[...].astype(F32)
+
+    @pl.when(me > 0)
+    def _():
+        halo_in.wait_recv()
+        ext[:, pl.ds(0, 8), :] = halo[...].astype(F32)
+
+    @pl.when(me == 0)
+    def _():
+        ext[:, pl.ds(0, 8), :] = jnp.zeros((3, 8, ext.shape[2]), F32)
+
+    @pl.when(me < count - 1)
+    def _():
+        next_in.wait_recv()
+        ext[pl.ds(1, 2), pl.ds(8 + TILE, 8), :] = halo_next[...].astype(F32)
+
+    @pl.when(me == count - 1)
+    def _():
+        ext[pl.ds(1, 2), pl.ds(8 + TILE, 8), :] = jnp.zeros((2, 8, width), F32)
+
+    for i in range(3):
+        number = TILE + 8 if i else TILE
+        for q in range(width // TILE):
+            lanes = pl.ds(q * TILE, TILE)
+            total = None
+            for j in range(reach + 1):
+                term = taps[i, pl.ds(j, 1), lanes] * ext[i, pl.ds(8 - j, number), lanes]
+                total = term if total is None else total + term
+            local_qkv[i, pl.ds(0, number), lanes] = total
 
     strips = [pl.ds(q * TILE, TILE) for q in range(width // TILE)]
 

time: 52 us -> 50.8 us (0.977)
  Pallas kernels: 51.3 us -> 49.7 us
    pallas_call x1, Pallas kernels: 50.4 us -> 48.8 us  [local(): pl.pallas_call(block_kernel, out_shape=[jax.ShapeDtypeStruct(cotangent.sh...]
where the time goes in v8:
time: 50.8 us; the launch traced here: 50.4 us
  Pallas kernels  49.7 us (98%)
  between operations  0.64 us (1%)
    pallas_call x1, Pallas kernels, local(): pl.pallas_call(block_kernel, out_shape=[jax.ShapeDtypeStruct(cotangent.sh...  48.8 us

profile of v8, /device:TPU:6, one launch (start us, length us, event | category | flops | bytes accessed | tf_op | source)
XLA Modules:
  0.0 50.4 jit_solution(16972456104736254872)
XLA Ops:
  0.6 48.8 %shard_map.93 = (bf16[128,512]{1,0:T(8,128)(2,1)S(1)}, bf16[3,128,512]{2,1,0:T(8,128)(2,1)S(1)}, bf16[128,512]{1,0:T(8,128)(2,1)S(1)}, f32[3,7,512]{2,1,0:T(8,128)S(1)}) custom-call(bf16[3,128,512]{2,1,0:T(8,128)(2,1)} %streams_hbm.1, bf16[128,512]{1,0:T(8,128)(2,1)} %filters_hbm.1, bf16[128,512]{1,0:T(8,128)(2,1)} %cot_hbm.1, f32[3,7,512]{2,1,0:T(8,128)} %taps_hbm.1, ...), custom_call_target="tpu_custom_call" | custom-call | tf_op jit(solution)/shard_map/pallas_call | solution.py:444
  49.5 0.9 %shard_map.94 = (bf16[128,512]{1,0:T(8,128)(2,1)}, bf16[3,128,512]{2,1,0:T(8,128)(2,1)}, bf16[128,512]{1,0:T(8,128)(2,1)}, f32[3,7,512]{2,1,0:T(8,128)}) custom-call(bf16[128,512]{1,0:T(8,128)(2,1)S(1)} %get-tuple-element.8.refs_0_, bf16[3,128,512]{2,1,0:T(8,128)(2,1)S(1)} %get-tuple-element.9.refs_1_, bf16[128,512]{1,0:T(8,128)(2,1)S(1)} %get-tuple-element.10.refs_2_, ...), custom_call_target="tpu_custom_call" | custom-call | tf_op jit(solution)/shard_map/pallas_call | solution.py:459
